TPU v7x, 32 devices: a whole 2x2x4 slice. The times are simulated.
32 devices in a mesh: row: 4 (over y, x), col: 8 (over z, core).
Axes of the slice: x: 2, y: 2, z: 4, core: 2. Of those that a mesh axis runs over, the one named last changes fastest.
Arguments:
- perturbations: float32 [512, 4096], P('row', 'col'), may hold values from -200 to 200
- probes: float32 [4096, 128], P(('col', 'row')), may hold values from -6 to 6
Outputs:
- localized: float32 [4096, 2048], P('col', 'row')
- sampled: float32 [4096, 128], P(('col', 'row'))
All inputs are finite; a program needn't handle non-finite values.
Results may differ from a plain program's by a relative error of at most 0.00013.
Values sent between devices are 32-bit elements; how exact they have to be, the bound alone decides.
No kernel may reach another device: no remote copies, remote signals or barrier semaphores. Data moves between devices by JAX's collectives and lax.ppermute only.
A program may use at most 128 MiB of HBM per device.

v0:
```python
import functools
import math

import jax
import jax.numpy as jnp
from jax import lax
from jax.experimental import pallas as pl
from jax.experimental.pallas import tpu as pltpu
from jax.sharding import PartitionSpec as P


EPSILON = 1e-06
POWER_TERMS = (
    2.0 / math.pi - 4.0 / (3.0 * math.pi) - 4.0 / (15.0 * math.pi) - 4.0 / (35.0 * math.pi),
    8.0 / (3.0 * math.pi) + 32.0 / (15.0 * math.pi) + 72.0 / (35.0 * math.pi),
    -32.0 / (15.0 * math.pi) - 192.0 / (35.0 * math.pi),
    128.0 / (35.0 * math.pi),
)
EXTRA_ROWS = 8
VMEM = pl.BlockSpec(memory_space=pltpu.VMEM)
SMEM = pl.BlockSpec(memory_space=pltpu.SMEM)
ANY = pl.BlockSpec(memory_space=pl.ANY)
NN = (((1,), (0,)), ((), ()))
NT = (((1,), (1,)), ((), ()))


def col_shift(block, step):
    count = lax.axis_size("col")
    return lax.ppermute(block, "col", [((i + step) % count, i) for i in range(count)])


def core_swap(block):
    return lax.ppermute(block, "col", [(i ^ 1, i) for i in range(lax.axis_size("col"))])


def row_xor(block, mask):
    return lax.ppermute(block, "row", [(i ^ mask, i) for i in range(lax.axis_size("row"))])


def vmem_limit(*arrays, scratch=0):
    held = sum(math.prod(a.shape) * a.dtype.itemsize for a in arrays) + scratch
    return pltpu.CompilerParams(vmem_limit_bytes=min(held + (4 << 20), 60 << 20))


def split(value):
    high = value.astype(jnp.bfloat16)
    return high, (value - high.astype(jnp.float32)).astype(jnp.bfloat16)


def dot(a, b, dims):
    return lax.dot_general(a, b, dims, preferred_element_type=jnp.float32)


def normalize(pieces):
    members = sum(p.shape[0] for p in pieces)
    x = jnp.concatenate([p[...] for p in pieces], 0)
    centered = x - jnp.sum(x, 0, keepdims=True) / members
    spread = jnp.sqrt(jnp.sum(centered * centered, 0, keepdims=True) + EPSILON)
    return centered * (1.0 / spread)


def gram_block(offset, left_high, left_low, normed, high_ref, low_ref, square_ref, window):
    n = normed.shape[1]
    high, low = split(normed)
    part = dot(left_high, high, NN) + dot(left_high, low, NN) + dot(left_low, high, NN)
    ahead = lax.broadcasted_iota(jnp.int32, (n, n), 1) - lax.broadcasted_iota(jnp.int32, (n, n), 0)
    distance = jnp.abs(ahead + offset * n).astype(jnp.float32)
    tapered = part * jnp.maximum(0.0, 1.0 - distance * (1.0 / window))
    high, low = split(tapered)
    high_ref[...] = high
    low_ref[...] = low
    square_ref[...] = jnp.sum((tapered * tapered).reshape(n // 8, 8, n), 0)


def own_kernel(count, window, *refs):
    pieces = refs[:count]
    left_high_ref, left_low_ref, high_ref, low_ref, square_ref, normed_ref = refs[count:]
    normed = normalize(pieces)
    normed_ref[...] = normed
    left_high, left_low = split(normed.T)
    left_high_ref[...] = left_high
    left_low_ref[...] = left_low
    gram_block(0, left_high, left_low, normed, high_ref, low_ref, square_ref, window)


def other_kernel(count, window, raw, *refs):
    offset_ref, left_high_ref, left_low_ref = refs[:3]
    pieces = refs[3 : 3 + count]
    high_ref, low_ref, square_ref = refs[3 + count :]
    normed = normalize(pieces) if raw else pieces[0][...]
    gram_block(
        offset_ref[0], left_high_ref[...], left_low_ref[...], normed,
        high_ref, low_ref, square_ref, window,
    )


def own_gram(pieces, window):
    n = pieces[0].shape[1]
    members = sum(p.shape[0] for p in pieces)
    left = jax.ShapeDtypeStruct((n, members), jnp.bfloat16)
    band = jax.ShapeDtypeStruct((n, n), jnp.bfloat16)
    outs = (left, left, band, band, jax.ShapeDtypeStruct((8, n), jnp.float32), jax.ShapeDtypeStruct((members, n), jnp.float32))
    return pl.pallas_call(
        functools.partial(own_kernel, len(pieces), window),
        out_shape=outs,
        compiler_params=vmem_limit(*pieces, *outs, scratch=16 * n * (n + members)),
        in_specs=[VMEM] * len(pieces),
        out_specs=[VMEM] * 6,
        name="own_gram",
        cost_estimate=pl.CostEstimate(flops=6 * n * n * members, bytes_accessed=4 * n * members, transcendentals=0),
    )(*pieces)


def other_gram(offset, left, pieces, window, raw=True):
    n = pieces[0].shape[1]
    members = sum(p.shape[0] for p in pieces)
    band = jax.ShapeDtypeStruct((n, n), jnp.bfloat16)
    outs = (band, band, jax.ShapeDtypeStruct((8, n), jnp.float32))
    return pl.pallas_call(
        functools.partial(other_kernel, len(pieces), window, raw),
        out_shape=outs,
        compiler_params=vmem_limit(*left, *pieces, *outs, scratch=16 * n * (n + members)),
        in_specs=[SMEM] + [VMEM] * (2 + len(pieces)),
        out_specs=[VMEM] * 3,
        cost_estimate=pl.CostEstimate(flops=6 * n * n * members, bytes_accessed=4 * n * members, transcendentals=0),
    )(offset, *left, *pieces)


def band_product(bands, windows, probes):
    n = bands[0][0].shape[0]
    wide = jnp.zeros((2 * probes, n), jnp.float32)
    narrow = jnp.zeros((probes, n), jnp.float32)
    for (high_ref, low_ref), w_ref in zip(bands, windows):
        high, low = split(w_ref[:probes, :])
        band_high = high_ref[...]
        wide += dot(jnp.concatenate([high, low], 0), band_high, NT)
        narrow += dot(high, low_ref[...], NT)
    return wide[:probes] + wide[probes:] + narrow


def unpack(refs, slots):
    bands = list(zip(refs[:slots], refs[slots : 2 * slots]))
    return bands, refs[2 * slots : 3 * slots], refs[3 * slots :]


def first_kernel(slots, probes, *refs):
    bands, windows, rest = unpack(refs, slots)
    squares, y_ref = rest[:slots], rest[slots]
    n = y_ref.shape[1]
    total = squares[0][...]
    for square in squares[1:]:
        total += square[...]
    y_ref[:probes, :] = band_product(bands, windows, probes)
    y_ref[probes:, :] = jnp.broadcast_to(jnp.sum(jnp.sum(total, 1, keepdims=True), 0, keepdims=True), (EXTRA_ROWS, n))


def second_kernel(slots, probes, reach_pairs, *refs):
    bands, windows, (y_ref,) = unpack(refs, slots)
    y_ref[:probes, :] = band_product(bands, windows, probes)
    here = [windows[k][probes : probes + 1, :] for k in range(2 * reach_pairs + 1)]
    zero = jnp.zeros_like(here[0])
    y_ref[probes : probes + 1, :] = functools.reduce(jnp.add, here)
    y_ref[probes + 1 : probes + 2, :] = functools.reduce(jnp.add, here[reach_pairs + 1 :], zero)
    y_ref[probes + 2 : probes + 3, :] = functools.reduce(jnp.add, here[1:reach_pairs], zero)
    y_ref[probes + 3 :, :] = jnp.zeros((EXTRA_ROWS - 3, y_ref.shape[1]), jnp.float32)


def last_kernel(slots, probes, reach_pairs, state_count, *refs):
    bands, windows, (w0_ref, y1_ref, y2_ref, out_ref) = unpack(refs, slots)
    y3 = band_product(bands, windows, probes)
    sums = y2_ref[probes : probes + 1, :] + windows[2 * reach_pairs][probes + 1 : probes + 2, :]
    sums += windows[0][probes + 2 : probes + 3, :]
    for row in range(probes, probes + 3):
        sums += windows[-1][row : row + 1, :]
    scale = sums / state_count
    total = POWER_TERMS[0] * w0_ref[...]
    total += POWER_TERMS[1] * (y1_ref[:probes, :] / scale)
    total += POWER_TERMS[2] * (y2_ref[:probes, :] / scale / scale)
    total += POWER_TERMS[3] * (y3 / scale / scale / scale)
    out_ref[...] = jnp.sqrt(scale) * total


def skew_kernel(slots, *refs):
    picks_ref, out_ref = refs[0], refs[1 + 2 * slots]
    high_scratch, low_scratch, sem = refs[2 + 2 * slots :]
    n = out_ref.shape[0]
    for place in range(2):
        for k in range(slots):
            @pl.when(picks_ref[place] == k)
            def _(place=place, k=k):
                a = pltpu.make_async_copy(refs[1 + k], high_scratch.at[place], sem.at[0])
                b = pltpu.make_async_copy(refs[1 + slots + k], low_scratch.at[place], sem.at[1])
                a.start()
                b.start()
                a.wait()
                b.wait()

    group = 8
    flip = group - 1 - lax.broadcasted_iota(jnp.int32, (group, n), 0)
    row = lax.broadcasted_iota(jnp.int32, (2 * group, n), 0)
    lane = lax.broadcasted_iota(jnp.int32, (2 * group, n), 1)
    for start in range(0, n, 2 * group):
        rows = slice(start, start + 2 * group)
        near = high_scratch[0, rows, :].astype(jnp.float32) + low_scratch[0, rows, :].astype(jnp.float32)
        far = high_scratch[1, rows, :].astype(jnp.float32) + low_scratch[1, rows, :].astype(jnp.float32)
        value = jnp.where(lane >= row + start, near, far)
        for half in (0, group):
            part = jnp.take_along_axis(value[half : half + group], flip, axis=0)
            part = pltpu.roll(part, (2 * n - start - half - group + 1) % n, 1, stride=1, stride_axis=0)
            out_ref[start + half : start + half + group, :] = jnp.take_along_axis(part, flip, axis=0)


def skewed(picks, bands):
    slots = len(bands)
    n = bands[0][0].shape[0]
    return pl.pallas_call(
        functools.partial(skew_kernel, slots),
        out_shape=jax.ShapeDtypeStruct((n, n), jnp.float32),
        in_specs=[SMEM] + [ANY] * (2 * slots),
        out_specs=VMEM,
        compiler_params=vmem_limit(scratch=12 * n * n),
        scratch_shapes=[
            pltpu.VMEM((2, n, n), jnp.bfloat16),
            pltpu.VMEM((2, n, n), jnp.bfloat16),
            pltpu.SemaphoreType.DMA((2,)),
        ],
        name="skew_out",
        cost_estimate=pl.CostEstimate(flops=40 * n * n, bytes_accessed=12 * n * n, transcendentals=0),
    )(picks, *[b[0] for b in bands], *[b[1] for b in bands])


def step_call(kernel, bands, windows, extra, rows):
    n = bands[0][0].shape[0]
    operands = [b[0] for b in bands] + [b[1] for b in bands] + list(windows) + list(extra)
    return pl.pallas_call(
        kernel,
        out_shape=jax.ShapeDtypeStruct((rows, n), jnp.float32),
        compiler_params=vmem_limit(*operands, scratch=32 * rows * n),
        in_specs=[VMEM] * len(operands),
        out_specs=VMEM,
        cost_estimate=pl.CostEstimate(flops=6 * n * n * rows * len(bands), bytes_accessed=4 * n * n * len(bands), transcendentals=0),
    )(*operands)


def on_device(perturbations, probes):
    row_count = lax.axis_size("row")
    col_count = lax.axis_size("col")
    row_index = lax.axis_index("row")
    core = lax.axis_index("col") % 2
    n = perturbations.shape[1]
    state_count = n * col_count
    window = state_count // 4
    reach = col_count // 4
    pairs = reach // 2
    probe_count = probes.shape[1] // row_count
    sides = [t for t in range(-pairs, pairs + 1) if t != 0]

    def window_of(held, outer):
        inner = [core_swap(held[t]) for t in range(1 - pairs, pairs)]
        return [held[t] for t in range(-pairs, pairs + 1)] + inner + [core_swap(outer)]

    def far_pick(held):
        return jnp.where(core == 1, held[-pairs], held[pairs])

    def exchange(block):
        return {0: block} | {t: col_shift(block, 2 * t) for t in sides}

    last_mask = row_count - 1
    blocks = {0: {0: perturbations}}
    for t in sides:
        blocks[t] = {0: col_shift(perturbations, 2 * t)}
    for mask in range(last_mask, 0, -1):
        blocks[0][mask] = row_xor(perturbations, mask)
    w0 = lax.all_to_all(probes.T, "row", split_axis=0, concat_axis=1, tiled=True)
    held = exchange(w0)
    windows = window_of(held, far_pick(held))
    for t in sides:
        for mask in range(1, last_mask):
            blocks[t][mask] = row_xor(blocks[t][0], mask)
        blocks[t][last_mask] = col_shift(blocks[0][last_mask], 2 * t)

    partner = 1 - 2 * core
    offsets = [2 * t for t in range(-pairs, pairs + 1)]
    offsets += [2 * t + partner for t in range(1 - pairs, pairs)] + [-partner * (reach - 1)]
    slots = len(offsets)
    bands = {}
    squares = {}
    left_high, left_low, high, low, square, normed = own_gram([blocks[0][k] for k in range(row_count)], window)
    left = (left_high, left_low)
    bands[pairs], squares[pairs] = (high, low), square

    def add_slot(k, pieces, raw=True):
        offset = jnp.asarray(offsets[k], jnp.int32).reshape(1)
        high, low, square = other_gram(offset, left, pieces, window, raw)
        bands[k], squares[k] = (high, low), square

    for t in range(1 - pairs, pairs):
        if t == 0:
            add_slot(3 * pairs, [core_swap(normed)], raw=False)
        else:
            pieces = [core_swap(blocks[t][k]) for k in range(row_count)]
            add_slot(3 * pairs + t, pieces)
    far = [core_swap(far_pick({t: blocks[t][k] for t in sides})) for k in range(row_count)]
    for t in sides:
        add_slot(pairs + t, [blocks[t][k] for k in range(row_count)])
    add_slot(slots - 1, far)
    bands = [bands[k] for k in range(slots)]
    squares = [squares[k] for k in range(slots)]

    def slot_of(offset):
        inner = 3 * pairs + (offset - partner) // 2
        odd = jnp.where(offset == -partner * (reach - 1), slots - 1, inner)
        return jnp.where(offset % 2 == 0, offset // 2 + pairs, odd)

    near = row_index - reach
    picks = jnp.stack([slot_of(near), slot_of(near + 1)]).astype(jnp.int32)
    localized = skewed(picks, bands)

    rows = probe_count + EXTRA_ROWS
    y1 = step_call(functools.partial(first_kernel, slots, probe_count), bands, windows, squares, rows)
    held = exchange(y1)
    windows = window_of(held, far_pick(held))
    y2 = step_call(functools.partial(second_kernel, slots, probe_count, pairs), bands, windows, [], rows)
    held = exchange(y2)
    row = lax.broadcasted_iota(jnp.int32, y2.shape, 0) - probe_count
    tail = jnp.where(row == 0, y2, jnp.where(row == 1, held[pairs], held[-pairs]))
    windows = window_of(held, jnp.where(row < 0, far_pick(held), tail))
    sampled = step_call(
        functools.partial(last_kernel, slots, probe_count, pairs, state_count), bands, windows, [w0, y1, y2], probe_count
    )
    sampled = lax.all_to_all(sampled, "row", split_axis=1, concat_axis=0, tiled=True).T
    return (localized, sampled)


def solution(mesh):
    return jax.shard_map(
        on_device,
        mesh=mesh,
        in_specs=(P("row", "col"), P(("col", "row"), None)),
        out_specs=(P("col", "row"), P(("col", "row"), None)),
        check_vma=False,
    )
```

profile of v0, /device:TPU:0, one launch (start us, length us, event | category | flops | bytes accessed | tf_op | source)
XLA Modules:
  0.0 94.9 jit_solution(18080319823822618485)
XLA Ops:
  2.2 5.2 %all-to-all-start = ((f32[4,32,128]{2,1,0:T(8,128)}), f32[4,32,128]{2,1,0:T(8,128)S(1)}, u32[]{:S(2)}, u32[]{:S(2)}) async-start(f32[4,32,128]{2,1,0:T(8,128)} %bitcast.5), calls=%async_computation | async-start | bytes 131072 | tf_op jit(solution)/shard_map/all_to_all | solution.py:274
  9.0 2.2 %collective-permute-start.7 = (f32[128,512]{1,0:T(8,128)S(1)}, f32[128,512]{1,0:T(8,128)S(1)}, u32[]{:S(2)}, u32[]{:S(2)}) collective-permute-start(f32[128,512]{1,0:T(8,128)S(1)} %copy-done.14), channel_id=1, source_target_pairs={{2,0},{3,1},{4,2},{5,3},{6,4},{7,5},{0,6},{1,7},{10,8},{11,9},{12,... | collective-permute-start | bytes 786440 | tf_op jit(solution)/shard_map/ppermute | solution.py:29
  11.3 2.9 %collective-permute-start.2 = (f32[128,512]{1,0:T(8,128)S(1)}, f32[128,512]{1,0:T(8,128)S(1)}, u32[]{:S(2)}, u32[]{:S(2)}) collective-permute-start(f32[128,512]{1,0:T(8,128)S(1)} %copy-done.14), channel_id=1, source_target_pairs={{24,0},{16,8},{8,16},{0,24},{25,1},{17,9},{9,17},{1,25},{26,2},{18... | collective-permute-start | bytes 786440 | tf_op jit(solution)/shard_map/ppermute | solution.py:37
  14.8 3.7 %collective-permute-done.3.refs_3_ = f32[128,512]{1,0:T(8,128)S(1)} collective-permute-done((f32[128,512]{1,0:T(8,128)S(1)}, f32[128,512]{1,0:T(8,128)S(1)}, u32[]{:S(2)}, u32[]{:S(2)}) %collective-permute-start.3) | collective-permute-done | bytes 262176 | tf_op jit(solution)/shard_map/ppermute | solution.py:29
  18.5 2.0 %collective-permute-start.4 = (f32[128,512]{1,0:T(8,128)S(1)}, f32[128,512]{1,0:T(8,128)S(1)}, u32[]{:S(2)}, u32[]{:S(2)}) collective-permute-start(f32[128,512]{1,0:T(8,128)S(1)} %collective-permute-done.3.refs_3_), channel_id=1, source_target_pairs={{8,0},{0,8},{24,16},{16,24},{9,1},{1,9},{25,17},{17,25},{10,2},{2,... | collective-permute-start | bytes 786440 | tf_op jit(solution)/shard_map/ppermute | solution.py:37
  20.5 1.6 %collective-permute-done.7.refs_3_ = f32[128,512]{1,0:T(8,128)S(1)} collective-permute-done((f32[128,512]{1,0:T(8,128)S(1)}, f32[128,512]{1,0:T(8,128)S(1)}, u32[]{:S(2)}, u32[]{:S(2)}) %collective-permute-start.7) | collective-permute-done | bytes 262176 | tf_op jit(solution)/shard_map/ppermute | solution.py:29
  22.1 1.7 %collective-permute-start.8 = (f32[128,512]{1,0:T(8,128)S(1)}, f32[128,512]{1,0:T(8,128)S(1)}, u32[]{:S(2)}, u32[]{:S(2)}) collective-permute-start(f32[128,512]{1,0:T(8,128)S(1)} %collective-permute-done.7.refs_3_), channel_id=1, source_target_pairs={{8,0},{0,8},{24,16},{16,24},{9,1},{1,9},{25,17},{17,25},{10,2},{2,... | collective-permute-start | bytes 786440 | tf_op jit(solution)/shard_map/ppermute | solution.py:37
  23.9 3.7 %collective-permute-done.refs_1_ = f32[128,512]{1,0:T(8,128)S(1)} collective-permute-done((f32[128,512]{1,0:T(8,128)S(1)}, f32[128,512]{1,0:T(8,128)S(1)}, u32[]{:S(2)}, u32[]{:S(2)}) %collective-permute-start) | collective-permute-done | bytes 262176 | tf_op jit(solution)/shard_map/ppermute | solution.py:37
  29.3 2.0 %collective-permute-start.9 = (f32[128,512]{1,0:T(8,128)S(1)}, f32[128,512]{1,0:T(8,128)S(1)}, u32[]{:S(2)}, u32[]{:S(2)}) collective-permute-start(f32[128,512]{1,0:T(8,128)S(1)} %collective-permute-done.7.refs_3_), channel_id=1, source_target_pairs={{16,0},{24,8},{0,16},{8,24},{17,1},{25,9},{1,17},{9,25},{18,2},{26... | collective-permute-start | bytes 786440 | tf_op jit(solution)/shard_map/ppermute | solution.py:37
  31.4 1.8 %collective-permute-done.4.refs_4_ = f32[128,512]{1,0:T(8,128)S(1)} collective-permute-done((f32[128,512]{1,0:T(8,128)S(1)}, f32[128,512]{1,0:T(8,128)S(1)}, u32[]{:S(2)}, u32[]{:S(2)}) %collective-permute-start.4) | collective-permute-done | bytes 262176 | tf_op jit(solution)/shard_map/ppermute | solution.py:37
  33.2 1.8 %collective-permute-start.10 = (f32[128,512]{1,0:T(8,128)S(1)}, f32[128,512]{1,0:T(8,128)S(1)}, u32[]{:S(2)}, u32[]{:S(2)}) collective-permute-start(f32[128,512]{1,0:T(8,128)S(1)} %collective-permute-done.2.refs_3_), channel_id=1, source_target_pairs={{2,0},{3,1},{4,2},{5,3},{6,4},{7,5},{0,6},{1,7},{10,8},{11,9},{12,... | collective-permute-start | bytes 786440 | tf_op jit(solution)/shard_map/ppermute | solution.py:29
  35.0 1.7 %collective-permute-done.8.refs_4_ = f32[128,512]{1,0:T(8,128)S(1)} collective-permute-done((f32[128,512]{1,0:T(8,128)S(1)}, f32[128,512]{1,0:T(8,128)S(1)}, u32[]{:S(2)}, u32[]{:S(2)}) %collective-permute-start.8) | collective-permute-done | bytes 262176 | tf_op jit(solution)/shard_map/ppermute | solution.py:37
  36.7 1.8 %collective-permute-done.5.refs_5_ = f32[128,512]{1,0:T(8,128)S(1)} collective-permute-done((f32[128,512]{1,0:T(8,128)S(1)}, f32[128,512]{1,0:T(8,128)S(1)}, u32[]{:S(2)}, u32[]{:S(2)}) %collective-permute-start.5) | collective-permute-done | bytes 262176 | tf_op jit(solution)/shard_map/ppermute | solution.py:37
  38.5 5.1 %collective-permute-done.9.refs_5_ = f32[128,512]{1,0:T(8,128)S(1)} collective-permute-done((f32[128,512]{1,0:T(8,128)S(1)}, f32[128,512]{1,0:T(8,128)S(1)}, u32[]{:S(2)}, u32[]{:S(2)}) %collective-permute-start.9) | collective-permute-done | bytes 262176 | tf_op jit(solution)/shard_map/ppermute | solution.py:37
  43.5 1.8 %collective-permute-start.17 = (f32[32,512]{1,0:T(8,128)S(1)}, f32[32,512]{1,0:T(8,128)S(1)}, u32[]{:S(2)}, u32[]{:S(2)}) collective-permute-start(f32[32,512]{1,0:T(8,128)S(1)} %copy_bitcast_fusion.refs_11_.refs_15_), channel_id=1, source_target_pairs={{2,0},{3,1},{4,2},{5,3},{6,4},{7,5},{0,6},{1,7},{10,8},{11,9},{12,... | collective-permute-start | bytes 196616 | tf_op jit(solution)/shard_map/ppermute | solution.py:29
  55.2 1.6 %shard_map.45.refs_11_.refs_16_ = f32[40,512]{1,0:T(8,128)S(1)} custom-call(bf16[512,512]{1,0:T(8,128)(2,1)S(1)} %get-tuple-element.22.refs_1_.refs_0_, bf16[512,512]{1,0:T(8,128)(2,1)S(1)} %get-tuple-element.23.refs_2_.refs_1_, bf16[512,512]{1,0:T(8,128)(2,1)S(1)} %get-tuple-element.24.refs_3_.refs_2_, ...), custom_call_target="tpu_custom_call" | custom-call | flops 314572800 | bytes 5242880 | tf_op jit(solution)/shard_map/pallas_call | solution.py:235
  58.1 2.6 %collective-permute-start.21 = (f32[40,512]{1,0:T(8,128)S(1)}, f32[40,512]{1,0:T(8,128)S(1)}, u32[]{:S(2)}, u32[]{:S(2)}) collective-permute-start(f32[40,512]{1,0:T(8,128)S(1)} %shard_map.45.refs_11_.refs_16_), channel_id=1, source_target_pairs={{2,0},{3,1},{4,2},{5,3},{6,4},{7,5},{0,6},{1,7},{10,8},{11,9},{12,... | collective-permute-start | bytes 245768 | tf_op jit(solution)/shard_map/ppermute | solution.py:29
  60.7 3.3 %collective-permute-done.20.refs_10_ = f32[40,512]{1,0:T(8,128)S(1)} collective-permute-done((f32[40,512]{1,0:T(8,128)S(1)}, f32[40,512]{1,0:T(8,128)S(1)}, u32[]{:S(2)}, u32[]{:S(2)}) %collective-permute-start.20) | collective-permute-done | bytes 81952 | tf_op jit(solution)/shard_map/ppermute | solution.py:29
  65.7 1.6 %shard_map.46.refs_11_.refs_17_ = f32[40,512]{1,0:T(8,128)S(1)} custom-call(bf16[512,512]{1,0:T(8,128)(2,1)S(1)} %get-tuple-element.22.refs_1_.refs_0_, bf16[512,512]{1,0:T(8,128)(2,1)S(1)} %get-tuple-element.23.refs_2_.refs_1_, bf16[512,512]{1,0:T(8,128)(2,1)S(1)} %get-tuple-element.24.refs_3_.refs_2_, ...), custom_call_target="tpu_custom_call" | custom-call | flops 314572800 | bytes 5242880 | tf_op jit(solution)/shard_map/pallas_call | solution.py:235
  68.8 2.3 %collective-permute-start.25 = (f32[40,512]{1,0:T(8,128)S(1)}, f32[40,512]{1,0:T(8,128)S(1)}, u32[]{:S(2)}, u32[]{:S(2)}) collective-permute-start(f32[40,512]{1,0:T(8,128)S(1)} %shard_map.46.refs_11_.refs_17_), channel_id=1, source_target_pairs={{2,0},{3,1},{4,2},{5,3},{6,4},{7,5},{0,6},{1,7},{10,8},{11,9},{12,... | collective-permute-start | bytes 245768 | tf_op jit(solution)/shard_map/ppermute | solution.py:29
  71.1 3.3 %collective-permute-done.24.refs_10_ = f32[40,512]{1,0:T(8,128)S(1)} collective-permute-done((f32[40,512]{1,0:T(8,128)S(1)}, f32[40,512]{1,0:T(8,128)S(1)}, u32[]{:S(2)}, u32[]{:S(2)}) %collective-permute-start.24) | collective-permute-done | bytes 81952 | tf_op jit(solution)/shard_map/ppermute | solution.py:29
  81.3 2.6 %shard_map.47 = f32[32,512]{1,0:T(8,128)S(1)} custom-call(bf16[512,512]{1,0:T(8,128)(2,1)S(1)} %get-tuple-element.22.refs_1_.refs_0_, bf16[512,512]{1,0:T(8,128)(2,1)S(1)} %get-tuple-element.23.refs_2_.refs_1_, bf16[512,512]{1,0:T(8,128)(2,1)S(1)} %get-tuple-element.24.refs_3_.refs_2_, bf16[512,512]{1,0:T(8,128)(2,1)S(1)} %copy-done.7, ...), custom_call_target="tpu_custom_call" | custom-call | flops 251658240 | bytes 5242880 | tf_op jit(solution)/shard_map/pallas_call | solution.py:235
  84.5 3.3 %all-to-all-start.1 = ((f32[32,4,128]{2,0,1:T(8,128)}), f32[32,4,128]{2,0,1:T(8,128)S(1)}, u32[]{:S(2)}, u32[]{:S(2)}) async-start(f32[32,4,128]{2,0,1:T(8,128)} %copy_bitcast_fusion.1), calls=%async_computation.1 | async-start | bytes 131072 | tf_op jit(solution)/shard_map/all_to_all | solution.py:331
  92.0 2.1 %skew_out.1 = f32[512,512]{1,0:T(8,128)} custom-call(s32[2]{0:T(128)S(1)} %pad_add_fusion.refs_0_, bf16[512,512]{1,0:T(8,128)(2,1)S(1)} %get-tuple-element.22.refs_1_.refs_0_, bf16[512,512]{1,0:T(8,128)(2,1)S(1)} %get-tuple-element.23.refs_2_.refs_1_, bf16[512,512]{1,0:T(8,128)(2,1)S(1)} %get-tuple-element.24.refs_3_.refs_2_, ...), custom_call_target="tpu_custom_call" | custom-call | flops 10485760 | bytes 3145728 | tf_op jit(solution)/shard_map/skew_out/pallas_call | solution.py:216
  (89 shorter events, 32.2 us)
Async XLA Ops:
  2.2 12.5 %all-to-all-start = ((f32[4,32,128]{2,1,0:T(8,128)}), f32[4,32,128]{2,1,0:T(8,128)S(1)}, u32[]{:S(2)}, u32[]{:S(2)}) async-start(f32[4,32,128]{2,1,0:T(8,128)} %bitcast.5), calls=%async_computation | async-start | bytes 131072 | tf_op jit(solution)/shard_map/all_to_all | solution.py:274
  7.4 11.0 %collective-permute-start.3 = (f32[128,512]{1,0:T(8,128)S(1)}, f32[128,512]{1,0:T(8,128)S(1)}, u32[]{:S(2)}, u32[]{:S(2)}) collective-permute-start(f32[128,512]{1,0:T(8,128)S(1)} %copy-done.14), channel_id=1, source_target_pairs={{6,0},{7,1},{0,2},{1,3},{2,4},{3,5},{4,6},{5,7},{14,8},{15,9},{8,1... | collective-permute-start | bytes 786440 | tf_op jit(solution)/shard_map/ppermute | solution.py:29
  9.0 13.1 %collective-permute-start.7 = (f32[128,512]{1,0:T(8,128)S(1)}, f32[128,512]{1,0:T(8,128)S(1)}, u32[]{:S(2)}, u32[]{:S(2)}) collective-permute-start(f32[128,512]{1,0:T(8,128)S(1)} %copy-done.14), channel_id=1, source_target_pairs={{2,0},{3,1},{4,2},{5,3},{6,4},{7,5},{0,6},{1,7},{10,8},{11,9},{12,... | collective-permute-start | bytes 786440 | tf_op jit(solution)/shard_map/ppermute | solution.py:29
  11.3 12.6 %collective-permute-start.2 = (f32[128,512]{1,0:T(8,128)S(1)}, f32[128,512]{1,0:T(8,128)S(1)}, u32[]{:S(2)}, u32[]{:S(2)}) collective-permute-start(f32[128,512]{1,0:T(8,128)S(1)} %copy-done.14), channel_id=1, source_target_pairs={{24,0},{16,8},{8,16},{0,24},{25,1},{17,9},{9,17},{1,25},{26,2},{18... | collective-permute-start | bytes 786440 | tf_op jit(solution)/shard_map/ppermute | solution.py:37
  14.2 13.3 %collective-permute-start = (f32[128,512]{1,0:T(8,128)S(1)}, f32[128,512]{1,0:T(8,128)S(1)}, u32[]{:S(2)}, u32[]{:S(2)}) collective-permute-start(f32[128,512]{1,0:T(8,128)S(1)} %copy-done.14), channel_id=1, source_target_pairs={{8,0},{0,8},{24,16},{16,24},{9,1},{1,9},{25,17},{17,25},{10,2},{2,... | collective-permute-start | bytes 786440 | tf_op jit(solution)/shard_map/ppermute | solution.py:37
  14.8 12.8 %collective-permute-start.1 = (f32[128,512]{1,0:T(8,128)S(1)}, f32[128,512]{1,0:T(8,128)S(1)}, u32[]{:S(2)}, u32[]{:S(2)}) collective-permute-start(f32[128,512]{1,0:T(8,128)S(1)} %copy-done.14), channel_id=1, source_target_pairs={{16,0},{24,8},{0,16},{8,24},{17,1},{25,9},{1,17},{9,25},{18,2},{26... | collective-permute-start | bytes 786440 | tf_op jit(solution)/shard_map/ppermute | solution.py:37
  18.5 14.7 %collective-permute-start.4 = (f32[128,512]{1,0:T(8,128)S(1)}, f32[128,512]{1,0:T(8,128)S(1)}, u32[]{:S(2)}, u32[]{:S(2)}) collective-permute-start(f32[128,512]{1,0:T(8,128)S(1)} %collective-permute-done.3.refs_3_), channel_id=1, source_target_pairs={{8,0},{0,8},{24,16},{16,24},{9,1},{1,9},{25,17},{17,25},{10,2},{2,... | collective-permute-start | bytes 786440 | tf_op jit(solution)/shard_map/ppermute | solution.py:37
  22.1 14.5 %collective-permute-start.8 = (f32[128,512]{1,0:T(8,128)S(1)}, f32[128,512]{1,0:T(8,128)S(1)}, u32[]{:S(2)}, u32[]{:S(2)}) collective-permute-start(f32[128,512]{1,0:T(8,128)S(1)} %collective-permute-done.7.refs_3_), channel_id=1, source_target_pairs={{8,0},{0,8},{24,16},{16,24},{9,1},{1,9},{25,17},{17,25},{10,2},{2,... | collective-permute-start | bytes 786440 | tf_op jit(solution)/shard_map/ppermute | solution.py:37
  29.1 24.7 %collective-permute-start.11 = (f32[512,512]{1,0:T(8,128)S(1)}, f32[512,512]{1,0:T(8,128)S(1)}, u32[]{:S(2)}, u32[]{:S(2)}) collective-permute-start(f32[512,512]{1,0:T(8,128)S(1)} %get-tuple-element.25), channel_id=1, source_target_pairs={{1,0},{0,1},{3,2},{2,3},{5,4},{4,5},{7,6},{6,7},{9,8},{8,9},{11,10... | collective-permute-start | bytes 3145736 | tf_op jit(solution)/shard_map/ppermute | solution.py:33
  29.2 9.2 %collective-permute-start.5 = (f32[128,512]{1,0:T(8,128)S(1)}, f32[128,512]{1,0:T(8,128)S(1)}, u32[]{:S(2)}, u32[]{:S(2)}) collective-permute-start(f32[128,512]{1,0:T(8,128)S(1)} %collective-permute-done.3.refs_3_), channel_id=1, source_target_pairs={{16,0},{24,8},{0,16},{8,24},{17,1},{25,9},{1,17},{9,25},{18,2},{26... | collective-permute-start | bytes 786440 | tf_op jit(solution)/shard_map/ppermute | solution.py:37
  29.3 14.2 %collective-permute-start.9 = (f32[128,512]{1,0:T(8,128)S(1)}, f32[128,512]{1,0:T(8,128)S(1)}, u32[]{:S(2)}, u32[]{:S(2)}) collective-permute-start(f32[128,512]{1,0:T(8,128)S(1)} %collective-permute-done.7.refs_3_), channel_id=1, source_target_pairs={{16,0},{24,8},{0,16},{8,24},{17,1},{25,9},{1,17},{9,25},{18,2},{26... | collective-permute-start | bytes 786440 | tf_op jit(solution)/shard_map/ppermute | solution.py:37
  33.2 12.2 %collective-permute-start.10 = (f32[128,512]{1,0:T(8,128)S(1)}, f32[128,512]{1,0:T(8,128)S(1)}, u32[]{:S(2)}, u32[]{:S(2)}) collective-permute-start(f32[128,512]{1,0:T(8,128)S(1)} %collective-permute-done.2.refs_3_), channel_id=1, source_target_pairs={{2,0},{3,1},{4,2},{5,3},{6,4},{7,5},{0,6},{1,7},{10,8},{11,9},{12,... | collective-permute-start | bytes 786440 | tf_op jit(solution)/shard_map/ppermute | solution.py:29
  36.6 9.6 %collective-permute-start.6 = (f32[128,512]{1,0:T(8,128)S(1)}, f32[128,512]{1,0:T(8,128)S(1)}, u32[]{:S(2)}, u32[]{:S(2)}) collective-permute-start(f32[128,512]{1,0:T(8,128)S(1)} %collective-permute-done.2.refs_3_), channel_id=1, source_target_pairs={{6,0},{7,1},{0,2},{1,3},{2,4},{3,5},{4,6},{5,7},{14,8},{15,9},{8,1... | collective-permute-start | bytes 786440 | tf_op jit(solution)/shard_map/ppermute | solution.py:29
  38.5 9.0 %collective-permute-start.16 = (f32[32,512]{1,0:T(8,128)S(1)}, f32[32,512]{1,0:T(8,128)S(1)}, u32[]{:S(2)}, u32[]{:S(2)}) collective-permute-start(f32[32,512]{1,0:T(8,128)S(1)} %copy_bitcast_fusion.refs_11_.refs_15_), channel_id=1, source_target_pairs={{6,0},{7,1},{0,2},{1,3},{2,4},{3,5},{4,6},{5,7},{14,8},{15,9},{8,1... | collective-permute-start | bytes 196616 | tf_op jit(solution)/shard_map/ppermute | solution.py:29
  43.5 4.7 %collective-permute-start.17 = (f32[32,512]{1,0:T(8,128)S(1)}, f32[32,512]{1,0:T(8,128)S(1)}, u32[]{:S(2)}, u32[]{:S(2)}) collective-permute-start(f32[32,512]{1,0:T(8,128)S(1)} %copy_bitcast_fusion.refs_11_.refs_15_), channel_id=1, source_target_pairs={{2,0},{3,1},{4,2},{5,3},{6,4},{7,5},{0,6},{1,7},{10,8},{11,9},{12,... | collective-permute-start | bytes 196616 | tf_op jit(solution)/shard_map/ppermute | solution.py:29
  45.4 6.1 %collective-permute-start.12 = (f32[128,512]{1,0:T(8,128)S(1)}, f32[128,512]{1,0:T(8,128)S(1)}, u32[]{:S(2)}, u32[]{:S(2)}) collective-permute-start(f32[128,512]{1,0:T(8,128)S(1)} %broadcast_select_fusion.3), channel_id=1, source_target_pairs={{1,0},{0,1},{3,2},{2,3},{5,4},{4,5},{7,6},{6,7},{9,8},{8,9},{11,10... | collective-permute-start | bytes 786440 | tf_op jit(solution)/shard_map/ppermute | solution.py:33
  46.2 5.9 %collective-permute-start.13 = (f32[128,512]{1,0:T(8,128)S(1)}, f32[128,512]{1,0:T(8,128)S(1)}, u32[]{:S(2)}, u32[]{:S(2)}) collective-permute-start(f32[128,512]{1,0:T(8,128)S(1)} %broadcast_select_fusion.2), channel_id=1, source_target_pairs={{1,0},{0,1},{3,2},{2,3},{5,4},{4,5},{7,6},{6,7},{9,8},{8,9},{11,10... | collective-permute-start | bytes 786440 | tf_op jit(solution)/shard_map/ppermute | solution.py:33
  47.5 4.7 %collective-permute-start.14 = (f32[128,512]{1,0:T(8,128)S(1)}, f32[128,512]{1,0:T(8,128)S(1)}, u32[]{:S(2)}, u32[]{:S(2)}) collective-permute-start(f32[128,512]{1,0:T(8,128)S(1)} %broadcast_select_fusion.1), channel_id=1, source_target_pairs={{1,0},{0,1},{3,2},{2,3},{5,4},{4,5},{7,6},{6,7},{9,8},{8,9},{11,10... | collective-permute-start | bytes 786440 | tf_op jit(solution)/shard_map/ppermute | solution.py:33
  56.8 7.1 %collective-permute-start.20 = (f32[40,512]{1,0:T(8,128)S(1)}, f32[40,512]{1,0:T(8,128)S(1)}, u32[]{:S(2)}, u32[]{:S(2)}) collective-permute-start(f32[40,512]{1,0:T(8,128)S(1)} %shard_map.45.refs_11_.refs_16_), channel_id=1, source_target_pairs={{6,0},{7,1},{0,2},{1,3},{2,4},{3,5},{4,6},{5,7},{14,8},{15,9},{8,1... | collective-permute-start | bytes 245768 | tf_op jit(solution)/shard_map/ppermute | solution.py:29
  58.1 6.2 %collective-permute-start.21 = (f32[40,512]{1,0:T(8,128)S(1)}, f32[40,512]{1,0:T(8,128)S(1)}, u32[]{:S(2)}, u32[]{:S(2)}) collective-permute-start(f32[40,512]{1,0:T(8,128)S(1)} %shard_map.45.refs_11_.refs_16_), channel_id=1, source_target_pairs={{2,0},{3,1},{4,2},{5,3},{6,4},{7,5},{0,6},{1,7},{10,8},{11,9},{12,... | collective-permute-start | bytes 245768 | tf_op jit(solution)/shard_map/ppermute | solution.py:29
  67.3 7.2 %collective-permute-start.24 = (f32[40,512]{1,0:T(8,128)S(1)}, f32[40,512]{1,0:T(8,128)S(1)}, u32[]{:S(2)}, u32[]{:S(2)}) collective-permute-start(f32[40,512]{1,0:T(8,128)S(1)} %shard_map.46.refs_11_.refs_17_), channel_id=1, source_target_pairs={{6,0},{7,1},{0,2},{1,3},{2,4},{3,5},{4,6},{5,7},{14,8},{15,9},{8,1... | collective-permute-start | bytes 245768 | tf_op jit(solution)/shard_map/ppermute | solution.py:29
  68.8 6.0 %collective-permute-start.25 = (f32[40,512]{1,0:T(8,128)S(1)}, f32[40,512]{1,0:T(8,128)S(1)}, u32[]{:S(2)}, u32[]{:S(2)}) collective-permute-start(f32[40,512]{1,0:T(8,128)S(1)} %shard_map.46.refs_11_.refs_17_), channel_id=1, source_target_pairs={{2,0},{3,1},{4,2},{5,3},{6,4},{7,5},{0,6},{1,7},{10,8},{11,9},{12,... | collective-permute-start | bytes 245768 | tf_op jit(solution)/shard_map/ppermute | solution.py:29
  71.1 4.3 %collective-permute-start.26 = (f32[40,512]{1,0:T(8,128)S(1)}, f32[40,512]{1,0:T(8,128)}, u32[]{:S(2)}, u32[]{:S(2)}) collective-permute-start(f32[40,512]{1,0:T(8,128)S(1)} %shard_map.46.refs_11_.refs_17_), channel_id=1, source_target_pairs={{1,0},{0,1},{3,2},{2,3},{5,4},{4,5},{7,6},{6,7},{9,8},{8,9},{11,10... | collective-permute-start | bytes 245768 | tf_op jit(solution)/shard_map/ppermute | solution.py:33
  84.5 9.6 %all-to-all-start.1 = ((f32[32,4,128]{2,0,1:T(8,128)}), f32[32,4,128]{2,0,1:T(8,128)S(1)}, u32[]{:S(2)}, u32[]{:S(2)}) async-start(f32[32,4,128]{2,0,1:T(8,128)} %copy_bitcast_fusion.1), calls=%async_computation.1 | async-start | bytes 131072 | tf_op jit(solution)/shard_map/all_to_all | solution.py:331
  (21 other events, 91.6 us)
where the time goes:
time: 95.6 us; the launch traced here: 94.9 us
  starting transfers between devices  33.8 us (35%)
  waiting for transfers between devices  32.2 us (34%)
  Pallas kernels  15.7 us (16%)
  local copies, waits for them, and re-layouts  11.3 us (12%)
  other arithmetic  0.96 us (1%)
    ppermute x10, waiting for transfers between devices, col_shift(): lax.ppermute(block, 'col', [((i + step) % count, i) for i in range(count)])  15.3 us
    ppermute x10, starting transfers between devices, col_shift(): lax.ppermute(block, 'col', [((i + step) % count, i) for i in range(count)])  15.1 us
    ppermute x7, waiting for transfers between devices, row_xor(): lax.ppermute(block, 'row', [(i ^ mask, i) for i in range(lax.axis_size('r...  14 us
    unnamed x32, local copies, waits for them, and re-layouts  10.7 us
    ppermute x7, starting transfers between devices, row_xor(): lax.ppermute(block, 'row', [(i ^ mask, i) for i in range(lax.axis_size('r...  9.35 us
    pallas_call x4, Pallas kernels, other_gram(): pl.pallas_call(functools.partial(other_kernel, len(pieces), window, raw),...  6.14 us
    pallas_call x3, Pallas kernels, step_call(): pl.pallas_call(kernel, out_shape=jax.ShapeDtypeStruct((rows, n), jnp.floa...  5.85 us
    all_to_all x1, starting transfers between devices, on_device(): lax.all_to_all(probes.T, 'row', split_axis=0, concat_axis=1, tiled=True)  5.19 us
  transfers between devices with their start and end apart: 30, of which 16 were waited for; matrix products, arithmetic and copies ran while one was open for 1% of the time, Pallas kernels for 10%

commit v1 on v0

v1 whole, which is shorter than its diff:
```python
import functools
import math

import jax
import jax.numpy as jnp
from jax import lax
from jax.experimental import pallas as pl
from jax.experimental.pallas import tpu as pltpu
from jax.sharding import PartitionSpec as P


EPSILON = 1e-06
POWER_TERMS = (
    2.0 / math.pi - 4.0 / (3.0 * math.pi) - 4.0 / (15.0 * math.pi) - 4.0 / (35.0 * math.pi),
    8.0 / (3.0 * math.pi) + 32.0 / (15.0 * math.pi) + 72.0 / (35.0 * math.pi),
    -32.0 / (15.0 * math.pi) - 192.0 / (35.0 * math.pi),
    128.0 / (35.0 * math.pi),
)
EXTRA_ROWS = 8
VMEM = pl.BlockSpec(memory_space=pltpu.VMEM)
ANY = pl.BlockSpec(memory_space=pl.ANY)
NN = (((1,), (0,)), ((), ()))
NT = (((1,), (1,)), ((), ()))


def side_sign(side):
    span, late = side
    odd = (lax.axis_index("col") // 2 // span) & 1
    return (1 - 2 * late) * (2 * odd - 1)


def ring_swap(block, side):
    span, late = side
    count = lax.axis_size("col") // 2
    route = []
    for i in range(count):
        ahead = (i // span) % 2 != late
        other = (i + span if ahead else i - span) % count
        route += [(2 * i, 2 * other), (2 * i + 1, 2 * other + 1)]
    return lax.ppermute(block, "col", route)


def core_swap(block):
    return lax.ppermute(block, "col", [(i ^ 1, i) for i in range(lax.axis_size("col"))])


def row_xor(block, mask):
    return lax.ppermute(block, "row", [(i ^ mask, i) for i in range(lax.axis_size("row"))])


def vmem_limit(*arrays, scratch=0):
    held = sum(math.prod(a.shape) * a.dtype.itemsize for a in arrays) + scratch
    return pltpu.CompilerParams(vmem_limit_bytes=min(held + (4 << 20), 60 << 20))


def split(value):
    high = value.astype(jnp.bfloat16)
    return high, (value - high.astype(jnp.float32)).astype(jnp.bfloat16)


def dot(a, b, dims):
    return lax.dot_general(a, b, dims, preferred_element_type=jnp.float32)


def normalize(pieces):
    members = sum(p.shape[0] for p in pieces)
    x = jnp.concatenate([p[...] for p in pieces], 0)
    centered = x - jnp.sum(x, 0, keepdims=True) / members
    spread = jnp.sqrt(jnp.sum(centered * centered, 0, keepdims=True) + EPSILON)
    return centered * (1.0 / spread)


def device_core():
    return lax.axis_index("col") & 1


def gram_kernel(window, count, offset, raw, last, *refs):
    refs = list(refs)
    take = lambda k: [refs.pop(0) for _ in range(k)]
    own = offset is None
    left_high_ref, left_low_ref = (None, None) if own else take(2)
    pieces = take(count)
    (w_ref,) = take(1)
    sum_ref, squares_ref = (None, None) if own else take(2)
    high_ref, low_ref, y_ref, square_ref = take(4)
    normed = normalize(pieces) if raw else pieces[0][...]
    n = normed.shape[1]
    if own:
        left_high_out, left_low_out, normed_out = take(3)
        normed_out[...] = normed
        left_high, left_low = split(normed.T)
        left_high_out[...] = left_high
        left_low_out[...] = left_low
    else:
        left_high, left_low = left_high_ref[...], left_low_ref[...]
    high, low = split(normed)
    part = dot(left_high, high, NN) + dot(left_high, low, NN) + dot(left_low, high, NN)
    ahead = lax.broadcasted_iota(jnp.int32, (n, n), 1) - lax.broadcasted_iota(jnp.int32, (n, n), 0)
    shift = 0 if own else offset() * n
    distance = jnp.abs(ahead + shift).astype(jnp.float32)
    tapered = part * jnp.maximum(0.0, 1.0 - distance * (1.0 / window))
    high, low = split(tapered)
    high_ref[...] = high
    low_ref[...] = low
    square = jnp.sum((tapered * tapered).reshape(n // 8, 8, n), 0)
    product = band_product([(high_ref, low_ref)], [w_ref], w_ref.shape[0])
    if not own:
        square += squares_ref[...]
        product += sum_ref[...]
    probes = product.shape[0]
    y_ref[:probes, :] = product
    if last:
        total = jnp.sum(jnp.sum(square, 1, keepdims=True), 0, keepdims=True)
        y_ref[probes:, :] = jnp.broadcast_to(total, (EXTRA_ROWS, n))
    square_ref[...] = square


def gram(offset, left, pieces, w, carried, window, raw=True, last=False):
    own = offset is None
    n = pieces[0].shape[1]
    members = sum(p.shape[0] for p in pieces)
    probes = w.shape[0]
    band = jax.ShapeDtypeStruct((n, n), jnp.bfloat16)
    side = jax.ShapeDtypeStruct((n, members), jnp.bfloat16)
    y = jax.ShapeDtypeStruct((probes + (EXTRA_ROWS if last else 0), n), jnp.float32)
    outs = [band, band, y, jax.ShapeDtypeStruct((8, n), jnp.float32)]
    operands = [*pieces, w]
    if own:
        outs += [side, side, jax.ShapeDtypeStruct((members, n), jnp.float32)]
    else:
        operands = [*left, *operands, *carried]
    specs = [VMEM] * len(operands)
    return pl.pallas_call(
        functools.partial(gram_kernel, window, len(pieces), offset, raw, last),
        out_shape=tuple(outs),
        compiler_params=vmem_limit(*operands, *outs, scratch=16 * n * (n + members)),
        in_specs=specs,
        out_specs=[VMEM] * len(outs),
        cost_estimate=pl.CostEstimate(flops=6 * n * n * members, bytes_accessed=4 * n * members, transcendentals=0),
    )(*operands)


def band_product(bands, windows, probes):
    n = bands[0][0].shape[0]
    wide = jnp.zeros((2 * probes, n), jnp.float32)
    narrow = jnp.zeros((probes, n), jnp.float32)
    for (high_ref, low_ref), w_ref in zip(bands, windows):
        high, low = split(w_ref[:probes, :])
        band_high = high_ref[...]
        wide += dot(jnp.concatenate([high, low], 0), band_high, NT)
        narrow += dot(high, low_ref[...], NT)
    return wide[:probes] + wide[probes:] + narrow


def unpack(refs, slots):
    bands = list(zip(refs[:slots], refs[slots : 2 * slots]))
    return bands, refs[2 * slots : 3 * slots], refs[3 * slots :]


def second_kernel(slots, probes, reach_pairs, *refs):
    bands, windows, (y_ref,) = unpack(refs, slots)
    y_ref[:probes, :] = band_product(bands, windows, probes)
    here = [windows[k][probes : probes + 1, :] for k in range(2 * reach_pairs + 1)]
    ahead = jnp.zeros_like(here[0])
    behind = jnp.zeros_like(here[0])
    for span in range(1, reach_pairs + 1):
        first, second = here[2 * span - 1], here[2 * span]
        flag = side_sign((span, 0)) > 0
        ahead += jnp.where(flag, first, second)
        if span < reach_pairs:
            behind += jnp.where(flag, second, first)
    y_ref[probes : probes + 1, :] = functools.reduce(jnp.add, here)
    y_ref[probes + 1 : probes + 2, :] = ahead
    y_ref[probes + 2 : probes + 3, :] = behind
    y_ref[probes + 3 :, :] = jnp.zeros((EXTRA_ROWS - 3, y_ref.shape[1]), jnp.float32)


def last_kernel(slots, probes, reach_pairs, state_count, *refs):
    bands, windows, (w0_ref, y1_ref, y2_ref, *out_refs, total_ref) = unpack(refs, slots)
    y3 = band_product(bands, windows, probes)
    first, second = windows[2 * reach_pairs - 1], windows[2 * reach_pairs]
    flag = side_sign((reach_pairs, 0)) > 0
    sums = y2_ref[probes : probes + 1, :]
    sums += jnp.where(flag, first[probes + 1 : probes + 2, :], second[probes + 1 : probes + 2, :])
    sums += jnp.where(flag, second[probes + 2 : probes + 3, :], first[probes + 2 : probes + 3, :])
    for row in range(probes, probes + 3):
        sums += windows[-1][row : row + 1, :]
    scale = sums / state_count
    total = POWER_TERMS[0] * w0_ref[...]
    total += POWER_TERMS[1] * (y1_ref[:probes, :] / scale)
    total += POWER_TERMS[2] * (y2_ref[:probes, :] / scale / scale)
    total += POWER_TERMS[3] * (y3 / scale / scale / scale)
    total_ref[...] = jnp.sqrt(scale) * total
    width = out_refs[0].shape[1]
    for mask, out_ref in enumerate(out_refs):
        start = pl.multiple_of((lax.axis_index("row") ^ mask) * width, width)
        out_ref[...] = total_ref[:, pl.ds(start, width)]


def gather_kernel(*refs):
    *piece_refs, out_ref, stack_ref = refs
    height = piece_refs[0].shape[0]
    for mask, piece_ref in enumerate(piece_refs):
        start = pl.multiple_of((lax.axis_index("row") ^ mask) * height, height)
        stack_ref[pl.ds(start, height), :] = piece_ref[...]
    out_ref[...] = stack_ref[...].T


def split_kernel(probes_ref, *refs):
    *piece_refs, stack_ref = refs
    stack_ref[...] = probes_ref[...].T
    height = piece_refs[0].shape[0]
    for mask, piece_ref in enumerate(piece_refs):
        start = pl.multiple_of((lax.axis_index("row") ^ mask) * height, height)
        piece_ref[...] = stack_ref[pl.ds(start, height), :]


def join_kernel(*refs):
    *piece_refs, out_ref = refs
    width = piece_refs[0].shape[1]
    for mask, piece_ref in enumerate(piece_refs):
        start = pl.multiple_of((lax.axis_index("row") ^ mask) * width, width)
        out_ref[:, pl.ds(start, width)] = piece_ref[...]


def small_call(kernel, operands, outs, scratch=()):
    return pl.pallas_call(
        kernel,
        out_shape=outs,
        compiler_params=vmem_limit(*operands, *operands),
        in_specs=[VMEM] * len(operands),
        out_specs=jax.tree.map(lambda _: VMEM, outs),
        scratch_shapes=scratch,
    )(*operands)


def skew_kernel(offsets, reach, *refs):
    slots = len(offsets)
    out_ref = refs[2 * slots]
    high_scratch, low_scratch, sem = refs[1 + 2 * slots :]
    n = out_ref.shape[0]
    for place in range(2):
        wanted = lax.axis_index("row") - reach + place
        for k, offset in enumerate(offsets):
            @pl.when(wanted == offset())
            def _(place=place, k=k):
                a = pltpu.make_async_copy(refs[k], high_scratch.at[place], sem.at[0])
                b = pltpu.make_async_copy(refs[slots + k], low_scratch.at[place], sem.at[1])
                a.start()
                b.start()
                a.wait()
                b.wait()

    group = 8
    flip = group - 1 - lax.broadcasted_iota(jnp.int32, (group, n), 0)
    row = lax.broadcasted_iota(jnp.int32, (2 * group, n), 0)
    lane = lax.broadcasted_iota(jnp.int32, (2 * group, n), 1)
    for start in range(0, n, 2 * group):
        rows = slice(start, start + 2 * group)
        near = high_scratch[0, rows, :].astype(jnp.float32) + low_scratch[0, rows, :].astype(jnp.float32)
        far = high_scratch[1, rows, :].astype(jnp.float32) + low_scratch[1, rows, :].astype(jnp.float32)
        value = jnp.where(lane >= row + start, near, far)
        for half in (0, group):
            part = jnp.take_along_axis(value[half : half + group], flip, axis=0)
            part = pltpu.roll(part, (2 * n - start - half - group + 1) % n, 1, stride=1, stride_axis=0)
            out_ref[start + half : start + half + group, :] = jnp.take_along_axis(part, flip, axis=0)


def skewed(offsets, reach, bands):
    slots = len(bands)
    n = bands[0][0].shape[0]
    return pl.pallas_call(
        functools.partial(skew_kernel, offsets, reach),
        out_shape=jax.ShapeDtypeStruct((n, n), jnp.float32),
        in_specs=[ANY] * (2 * slots),
        out_specs=VMEM,
        compiler_params=vmem_limit(scratch=12 * n * n),
        scratch_shapes=[
            pltpu.VMEM((2, n, n), jnp.bfloat16),
            pltpu.VMEM((2, n, n), jnp.bfloat16),
            pltpu.SemaphoreType.DMA((2,)),
        ],
        name="skew_out",
        cost_estimate=pl.CostEstimate(flops=40 * n * n, bytes_accessed=12 * n * n, transcendentals=0),
    )(*[b[0] for b in bands], *[b[1] for b in bands])


def step_call(kernel, bands, windows, extra, outs, scratch=()):
    n = bands[0][0].shape[0]
    operands = [b[0] for b in bands] + [b[1] for b in bands] + list(windows) + list(extra)
    rows = windows[0].shape[0]
    return pl.pallas_call(
        kernel,
        out_shape=outs,
        compiler_params=vmem_limit(*operands, scratch=32 * rows * n),
        in_specs=[VMEM] * len(operands),
        out_specs=jax.tree.map(lambda _: VMEM, outs),
        scratch_shapes=scratch,
        cost_estimate=pl.CostEstimate(flops=6 * n * n * rows * len(bands), bytes_accessed=4 * n * n * len(bands), transcendentals=0),
    )(*operands)


def on_device(perturbations, probes):
    row_count = lax.axis_size("row")
    col_count = lax.axis_size("col")
    n = perturbations.shape[1]
    state_count = n * col_count
    window = state_count // 4
    reach = col_count // 4
    pairs = reach // 2
    probe_count = probes.shape[1] // row_count
    sides = [(span, late) for late in (0, 1) for span in range(1, pairs + 1)]
    keys = [None] + [(span, late) for span in range(1, pairs + 1) for late in (0, 1)]
    inner_keys = keys[: 2 * pairs - 1]
    last_pair = keys[-2:]

    def window_of(held, outer):
        inner = [core_swap(held[k]) for k in inner_keys]
        return [held[k] for k in keys] + inner + [core_swap(outer)]

    first_ahead = side_sign(last_pair[0]) > 0
    far_first = first_ahead == (device_core() == 0)
    perturbations, first_ahead, far_first = lax.optimization_barrier((perturbations, first_ahead, far_first))

    def far_pick(held):
        return jnp.where(far_first, held[last_pair[0]], held[last_pair[1]])

    def exchange(block):
        return {None: block} | {k: ring_swap(block, k) for k in sides}

    last_mask = row_count - 1
    blocks = {None: {0: perturbations}}
    for k in sides:
        blocks[k] = {0: ring_swap(perturbations, k)}
    for mask in range(last_mask, 0, -1):
        blocks[None][mask] = row_xor(perturbations, mask)
    piece = jax.ShapeDtypeStruct((probe_count, n // row_count), jnp.float32)
    turned = pltpu.VMEM((probes.shape[1], probes.shape[0]), jnp.float32)
    pieces = small_call(split_kernel, [probes], [piece] * row_count, [turned])
    pieces = [pieces[0]] + [row_xor(pieces[mask], mask) for mask in range(1, row_count)]
    w0 = small_call(join_kernel, pieces, jax.ShapeDtypeStruct((probe_count, n), jnp.float32))
    held = exchange(w0)
    windows = window_of(held, far_pick(held))
    for k in sides:
        for mask in range(1, last_mask):
            blocks[k][mask] = row_xor(blocks[k][0], mask)
        blocks[k][last_mask] = ring_swap(blocks[None][last_mask], k)

    def offset_of(key, inner):
        def offset():
            own = 0 if key is None else 2 * key[0] * side_sign(key)
            return own + (1 - 2 * device_core() if inner else 0)

        return offset

    offsets = [offset_of(k, False) for k in keys] + [offset_of(k, True) for k in inner_keys]
    offsets.append(lambda: (1 - reach) * (1 - 2 * device_core()))
    slots = len(offsets)
    bands = {}
    own_pieces = [blocks[None][mask] for mask in range(row_count)]
    high, low, y1, square, *left, normed = gram(None, None, own_pieces, windows[0], None, window)
    bands[0] = (high, low)

    def add_slot(k, pieces, carried, **kinds):
        high, low, *carried = gram(offsets[k], left, pieces, windows[k], carried, window, **kinds)
        bands[k] = (high, low)
        return carried

    def add_side(k, carried):
        return add_slot(keys.index(k), list(blocks[k].values()), carried)

    carried = [y1, square]
    near_block = core_swap(normed)
    far = [core_swap(far_pick({k: blocks[k][mask] for k in sides})) for mask in range(row_count)]
    for k in sides[:pairs]:
        carried = add_side(k, carried)
    for place, k in enumerate(inner_keys):
        slot = len(keys) + place
        if k is None:
            carried = add_slot(slot, [near_block], carried, raw=False)
        else:
            pieces = [core_swap(block) for block in blocks[k].values()]
            carried = add_slot(slot, pieces, carried)
    for k in sides[pairs:]:
        carried = add_side(k, carried)
    y1, _ = add_slot(slots - 1, far, carried, last=True)
    bands = [bands[k] for k in range(slots)]

    localized = skewed(offsets, reach, bands)

    held = exchange(y1)
    windows = window_of(held, far_pick(held))
    second = functools.partial(second_kernel, slots, probe_count, pairs)
    y2 = step_call(second, bands, windows, [], jax.ShapeDtypeStruct(y1.shape, y1.dtype))
    held = exchange(y2)
    row = lax.broadcasted_iota(jnp.int32, y2.shape, 0) - probe_count
    first, second = held[last_pair[0]], held[last_pair[1]]
    tail = jnp.where(row == 0, y2, jnp.where((row == 1) == first_ahead, first, second))
    windows = window_of(held, jnp.where(row < 0, far_pick(held), tail))
    pieces = step_call(
        functools.partial(last_kernel, slots, probe_count, pairs, state_count),
        bands, windows, [w0, y1, y2], [piece] * row_count,
        scratch=[pltpu.VMEM((probe_count, n), jnp.float32)],
    )
    pieces = [pieces[0]] + [row_xor(pieces[mask], mask) for mask in range(1, row_count)]
    sampled = small_call(gather_kernel, pieces, jax.ShapeDtypeStruct(probes.shape, jnp.float32), [turned])
    return (localized, sampled)


def solution(mesh):
    return jax.shard_map(
        on_device,
        mesh=mesh,
        in_specs=(P("row", "col"), P(("col", "row"), None)),
        out_specs=(P("col", "row"), P(("col", "row"), None)),
        check_vma=False,
    )
```

time: 95.6 us -> 87.3 us (0.913)
  local copies, waits for them, and re-layouts: 11.3 us -> 1.78 us
  waiting for transfers between devices: 32.2 us -> 34.8 us
    unnamed x32 -> x4, local copies, waits for them, and re-layouts: 10.7 us -> 1.78 us
    all_to_all x2 -> x0, starting transfers between devices: 8.48 us -> none  [the longest x1 5.19 us: on_device(): lax.all_to_all(probes.T, 'row', split_axis=0, concat_axis=1, tiled=True)]
    ppermute x7 -> x13, starting transfers between devices: 9.35 us -> 16.7 us  [row_xor(): lax.ppermute(block, 'row', [(i ^ mask, i) for i in range(lax.axis_size('r...]
    ppermute x10, waiting for transfers between devices: 15.3 us -> 19.4 us  [ring_swap(): return lax.ppermute(block, 'col', route)]
    ppermute x7 -> x13, waiting for transfers between devices: 14 us -> 12.8 us  [row_xor(): lax.ppermute(block, 'row', [(i ^ mask, i) for i in range(lax.axis_size('r...]
    pallas_call x9 -> x11, Pallas kernels: 15.7 us -> 15.2 us  [the longest x5 9.54 us: gram(): pl.pallas_call(functools.partial(gram_kernel, window, len(pieces), offset...]
  transfers between devices with their start and end apart: 30 -> 34, of which waited for: 16 -> 17; matrix products, arithmetic and copies ran while one was open for 1% -> 0% of each run, Pallas kernels for 10% -> 10%
where the time goes in v1:
time: 87.3 us; the launch traced here: 87.1 us
  waiting for transfers between devices  34.8 us (40%)
  starting transfers between devices  34.2 us (39%)
  Pallas kernels  15.2 us (17%)
  local copies, waits for them, and re-layouts  1.78 us (2%)
    ppermute x10, waiting for transfers between devices, ring_swap(): return lax.ppermute(block, 'col', route)  19.4 us
    ppermute x13, starting transfers between devices, row_xor(): lax.ppermute(block, 'row', [(i ^ mask, i) for i in range(lax.axis_size('r...  16.7 us
    ppermute x10, starting transfers between devices, ring_swap(): return lax.ppermute(block, 'col', route)  16.1 us
    ppermute x13, waiting for transfers between devices, row_xor(): lax.ppermute(block, 'row', [(i ^ mask, i) for i in range(lax.axis_size('r...  12.8 us
    pallas_call x5, Pallas kernels, gram(): pl.pallas_call(functools.partial(gram_kernel, window, len(pieces), offset...  9.54 us
    pallas_call x2, Pallas kernels, step_call(): pl.pallas_call(kernel, out_shape=outs, compiler_params=vmem_limit(*operan...  3.3 us
    ppermute x11, waiting for transfers between devices, core_swap(): lax.ppermute(block, 'col', [(i ^ 1, i) for i in range(lax.axis_size('col'...  2.58 us
    unnamed x4, local copies, waits for them, and re-layouts  1.78 us
  transfers between devices with their start and end apart: 34, of which 17 were waited for; matrix products, arithmetic and copies ran while one was open for 0% of the time, Pallas kernels for 10%

profile of v1, /device:TPU:0, one launch (start us, length us, event | category | flops | bytes accessed | tf_op | source)
XLA Modules:
  0.0 87.1 jit_solution(5709416565356443035)
XLA Ops:
  1.6 3.0 %collective-permute-start.3 = (f32[32,128]{1,0:T(8,128)S(1)}, f32[32,128]{1,0:T(8,128)S(1)}, u32[]{:S(2)}, u32[]{:S(2)}) collective-permute-start(f32[32,128]{1,0:T(8,128)S(1)} %get-tuple-element.37), channel_id=1, source_target_pairs={{8,0},{0,8},{24,16},{16,24},{9,1},{1,9},{25,17},{17,25},{10,2},{2,... | collective-permute-start | bytes 49160 | tf_op jit(solution)/shard_map/ppermute | solution.py:48
  6.1 2.0 %collective-permute-start.11 = (f32[128,512]{1,0:T(8,128)}, f32[128,512]{1,0:T(8,128)S(1)}, u32[]{:S(2)}, u32[]{:S(2)}) collective-permute-start(f32[128,512]{1,0:T(8,128)} %refs_0_), channel_id=1, source_target_pairs={{0,2},{1,3},{2,0},{3,1},{4,6},{5,7},{6,4},{7,5},{8,10},{9,11},{10,... | collective-permute-start | bytes 786440 | tf_op jit(solution)/shard_map/ppermute | solution.py:40
  8.2 2.5 %collective-permute-start.6 = (f32[128,512]{1,0:T(8,128)}, f32[128,512]{1,0:T(8,128)S(1)}, u32[]{:S(2)}, u32[]{:S(2)}) collective-permute-start(f32[128,512]{1,0:T(8,128)} %refs_0_), channel_id=1, source_target_pairs={{0,6},{1,7},{2,4},{3,5},{4,2},{5,3},{6,0},{7,1},{8,14},{9,15},{10,... | collective-permute-start | bytes 786440 | tf_op jit(solution)/shard_map/ppermute | solution.py:40
  10.7 2.4 %collective-permute-start.2 = (f32[128,512]{1,0:T(8,128)}, f32[128,512]{1,0:T(8,128)S(1)}, u32[]{:S(2)}, u32[]{:S(2)}) collective-permute-start(f32[128,512]{1,0:T(8,128)} %refs_0_), channel_id=1, source_target_pairs={{24,0},{16,8},{8,16},{0,24},{25,1},{17,9},{9,17},{1,25},{26,2},{18... | collective-permute-start | bytes 786440 | tf_op jit(solution)/shard_map/ppermute | solution.py:48
  16.7 5.0 %collective-permute-done.6.refs_2_ = f32[128,512]{1,0:T(8,128)S(1)} collective-permute-done((f32[128,512]{1,0:T(8,128)}, f32[128,512]{1,0:T(8,128)S(1)}, u32[]{:S(2)}, u32[]{:S(2)}) %collective-permute-start.6) | collective-permute-done | bytes 262176 | tf_op jit(solution)/shard_map/ppermute | solution.py:40
  25.5 1.9 %shard_map.43 = (bf16[512,512]{1,0:T(8,128)(2,1)S(1)}, bf16[512,512]{1,0:T(8,128)(2,1)S(1)}, f32[32,512]{1,0:T(8,128)S(1)}, f32[8,512]{1,0:T(8,128)S(1)}, bf16[5...) custom-call(f32[128,512]{1,0:T(8,128)S(1)} %copy-done.1, ...), custom_call_target="tpu_custom_call" | custom-call | flops 805306368 | bytes 1048576 | tf_op jit(solution)/shard_map/pallas_call | solution.py:133
  30.9 4.4 %collective-permute-done.8.refs_4_ = f32[128,512]{1,0:T(8,128)S(1)} collective-permute-done((f32[128,512]{1,0:T(8,128)S(1)}, f32[128,512]{1,0:T(8,128)S(1)}, u32[]{:S(2)}, u32[]{:S(2)}) %collective-permute-start.8) | collective-permute-done | bytes 262176 | tf_op jit(solution)/shard_map/ppermute | solution.py:48
  35.3 1.5 %collective-permute-start.9 = (f32[128,512]{1,0:T(8,128)S(1)}, f32[128,512]{1,0:T(8,128)S(1)}, u32[]{:S(2)}, u32[]{:S(2)}) collective-permute-start(f32[128,512]{1,0:T(8,128)S(1)} %collective-permute-done.2.refs_3_), channel_id=1, source_target_pairs={{0,6},{1,7},{2,4},{3,5},{4,2},{5,3},{6,0},{7,1},{8,14},{9,15},{10,... | collective-permute-start | bytes 786440 | tf_op jit(solution)/shard_map/ppermute | solution.py:40
  36.9 4.9 %collective-permute-done.7.refs_3_ = f32[128,512]{1,0:T(8,128)S(1)} collective-permute-done((f32[128,512]{1,0:T(8,128)S(1)}, f32[128,512]{1,0:T(8,128)S(1)}, u32[]{:S(2)}, u32[]{:S(2)}) %collective-permute-start.7) | collective-permute-done | bytes 262176 | tf_op jit(solution)/shard_map/ppermute | solution.py:48
  43.9 1.7 %collective-permute-done.9.refs_5_ = f32[128,512]{1,0:T(8,128)S(1)} collective-permute-done((f32[128,512]{1,0:T(8,128)S(1)}, f32[128,512]{1,0:T(8,128)S(1)}, u32[]{:S(2)}, u32[]{:S(2)}) %collective-permute-start.9) | collective-permute-done | bytes 262176 | tf_op jit(solution)/shard_map/ppermute | solution.py:40
  46.4 2.3 %collective-permute-done.10.refs_6_ = f32[32,512]{1,0:T(8,128)S(1)} collective-permute-done((f32[32,512]{1,0:T(8,128)S(1)}, f32[32,512]{1,0:T(8,128)S(1)}, u32[]{:S(2)}, u32[]{:S(2)}) %collective-permute-start.10) | collective-permute-done | bytes 65568 | tf_op jit(solution)/shard_map/ppermute | solution.py:40
  48.8 1.9 %shard_map.44 = (bf16[512,512]{1,0:T(8,128)(2,1)S(1)}, bf16[512,512]{1,0:T(8,128)(2,1)S(1)}, f32[32,512]{1,0:T(8,128)S(1)}, f32[8,512]{1,0:T(8,128)S(1)}) custom-call(bf16[512,512]{1,0:T(8,128)(2,1)S(1)} %get-tuple-element.41.refs_0_, bf16[512,512]{1,0:T(8,128)(2,1)S(1)} %get-tuple-element.42.refs_1_, f32[128,512]{1,0:T(8,128)S(1)} %collective-permute-done.6.refs_2_, ...), custom_call_target="tpu_custom_call" | custom-call | flops 805306368 | bytes 1048576 | tf_op jit(solution)/shard_map/pallas_call | solution.py:133
  51.3 1.6 %shard_map.45 = (bf16[512,512]{1,0:T(8,128)(2,1)S(1)}, bf16[512,512]{1,0:T(8,128)(2,1)S(1)}, f32[32,512]{1,0:T(8,128)S(1)}, f32[8,512]{1,0:T(8,128)S(1)}) custom-call(bf16[512,512]{1,0:T(8,128)(2,1)S(1)} %get-tuple-element.41.refs_0_, bf16[512,512]{1,0:T(8,128)(2,1)S(1)} %get-tuple-element.42.refs_1_, f32[512,512]{1,0:T(8,128)S(1)} %collective-permute-done.16.refs_2_, ...), custom_call_target="tpu_custom_call" | custom-call | flops 805306368 | bytes 1048576 | tf_op jit(solution)/shard_map/pallas_call | solution.py:133
  52.9 1.9 %shard_map.46 = (bf16[512,512]{1,0:T(8,128)(2,1)S(1)}, bf16[512,512]{1,0:T(8,128)(2,1)S(1)}, f32[32,512]{1,0:T(8,128)S(1)}, f32[8,512]{1,0:T(8,128)S(1)}) custom-call(bf16[512,512]{1,0:T(8,128)(2,1)S(1)} %get-tuple-element.41.refs_0_, bf16[512,512]{1,0:T(8,128)(2,1)S(1)} %get-tuple-element.42.refs_1_, f32[128,512]{1,0:T(8,128)S(1)} %collective-permute-done.11.refs_2_, ...), custom_call_target="tpu_custom_call" | custom-call | flops 805306368 | bytes 1048576 | tf_op jit(solution)/shard_map/pallas_call | solution.py:133
  54.9 2.2 %shard_map.47 = (bf16[512,512]{1,0:T(8,128)(2,1)S(1)}, bf16[512,512]{1,0:T(8,128)(2,1)S(1)}, f32[40,512]{1,0:T(8,128)S(1)}, f32[8,512]{1,0:T(8,128)}) custom-call(bf16[512,512]{1,0:T(8,128)(2,1)S(1)} %get-tuple-element.41.refs_0_, bf16[512,512]{1,0:T(8,128)(2,1)S(1)} %get-tuple-element.42.refs_1_, f32[128,512]{1,0:T(8,128)S(1)} %collective-permute-done.18.refs_2_, ...), custom_call_target="tpu_custom_call" | custom-call | flops 805306368 | bytes 1048576 | tf_op jit(solution)/shard_map/pallas_call | solution.py:133
  57.1 3.4 %collective-permute-start.24 = (f32[40,512]{1,0:T(8,128)S(1)}, f32[40,512]{1,0:T(8,128)S(1)}, u32[]{:S(2)}, u32[]{:S(2)}) collective-permute-start(f32[40,512]{1,0:T(8,128)S(1)} %get-tuple-element.62.refs_10_.refs_16_), channel_id=1, source_target_pairs={{0,2},{1,3},{2,0},{3,1},{4,6},{5,7},{6,4},{7,5},{8,10},{9,11},{10,... | collective-permute-start | bytes 245768 | tf_op jit(solution)/shard_map/ppermute | solution.py:40
  60.5 1.8 %collective-permute-start.23 = (f32[40,512]{1,0:T(8,128)S(1)}, f32[40,512]{1,0:T(8,128)S(1)}, u32[]{:S(2)}, u32[]{:S(2)}) collective-permute-start(f32[40,512]{1,0:T(8,128)S(1)} %get-tuple-element.62.refs_10_.refs_16_), channel_id=1, source_target_pairs={{0,6},{1,7},{2,4},{3,5},{4,2},{5,3},{6,0},{7,1},{8,14},{9,15},{10,... | collective-permute-start | bytes 245768 | tf_op jit(solution)/shard_map/ppermute | solution.py:40
  63.6 3.3 %collective-permute-done.23.refs_11_ = f32[40,512]{1,0:T(8,128)S(1)} collective-permute-done((f32[40,512]{1,0:T(8,128)S(1)}, f32[40,512]{1,0:T(8,128)S(1)}, u32[]{:S(2)}, u32[]{:S(2)}) %collective-permute-start.23) | collective-permute-done | bytes 81952 | tf_op jit(solution)/shard_map/ppermute | solution.py:40
  68.2 1.6 %shard_map.48.refs_10_.refs_17_ = f32[40,512]{1,0:T(8,128)S(1)} custom-call(bf16[512,512]{1,0:T(8,128)(2,1)S(1)} %get-tuple-element.40.refs_0_, bf16[512,512]{1,0:T(8,128)(2,1)S(1)} %get-tuple-element.45.refs_1_, bf16[512,512]{1,0:T(8,128)(2,1)S(1)} %get-tuple-element.51.refs_2_, bf16[512,512]{1,0:T(8,128)(2,1)S(1)} %get-tuple-element.52.refs_3_, ...), custom_call_target="tpu_custom_call" | custom-call | flops 314572800 | bytes 5242880 | tf_op jit(solution)/shard_map/pallas_call | solution.py:292
  69.8 2.1 %collective-permute-start.27 = (f32[40,512]{1,0:T(8,128)S(1)}, f32[40,512]{1,0:T(8,128)S(1)}, u32[]{:S(2)}, u32[]{:S(2)}) collective-permute-start(f32[40,512]{1,0:T(8,128)S(1)} %shard_map.48.refs_10_.refs_17_), channel_id=1, source_target_pairs={{0,6},{1,7},{2,4},{3,5},{4,2},{5,3},{6,0},{7,1},{8,14},{9,15},{10,... | collective-permute-start | bytes 245768 | tf_op jit(solution)/shard_map/ppermute | solution.py:40
  72.0 2.4 %collective-permute-done.28.refs_12_ = f32[40,512]{1,0:T(8,128)S(1)} collective-permute-done((f32[40,512]{1,0:T(8,128)S(1)}, f32[40,512]{1,0:T(8,128)S(1)}, u32[]{:S(2)}, u32[]{:S(2)}) %collective-permute-start.28) | collective-permute-done | bytes 81952 | tf_op jit(solution)/shard_map/ppermute | solution.py:40
  74.4 2.1 %collective-permute-done.27.refs_11_ = f32[40,512]{1,0:T(8,128)S(1)} collective-permute-done((f32[40,512]{1,0:T(8,128)S(1)}, f32[40,512]{1,0:T(8,128)S(1)}, u32[]{:S(2)}, u32[]{:S(2)}) %collective-permute-start.27) | collective-permute-done | bytes 81952 | tf_op jit(solution)/shard_map/ppermute | solution.py:40
  77.9 1.7 %shard_map.49 = (f32[32,128]{1,0:T(8,128)S(1)}, f32[32,128]{1,0:T(8,128)S(1)}, f32[32,128]{1,0:T(8,128)S(1)}, f32[32,128]{1,0:T(8,128)S(1)}) custom-call(bf16[512,512]{1,0:T(8,128)(2,1)S(1)} %get-tuple-element.40.refs_0_, bf16[512,512]{1,0:T(8,128)(2,1)S(1)} %get-tuple-element.45.refs_1_, bf16[512,512]{1,0:T(8,128)(2,1)S(1)} %get-tuple-element.51.refs_2_, ...), custom_call_target="tpu_custom_call" | custom-call | flops 314572800 | bytes 5242880 | tf_op jit(solution)/shard_map/pallas_call | solution.py:292
  79.6 2.0 %collective-permute-start.31 = (f32[32,128]{1,0:T(8,128)S(1)}, f32[32,128]{1,0:T(8,128)S(1)}, u32[]{:S(2)}, u32[]{:S(2)}) collective-permute-start(f32[32,128]{1,0:T(8,128)S(1)} %get-tuple-element.65), channel_id=1, source_target_pairs={{8,0},{0,8},{24,16},{16,24},{9,1},{1,9},{25,17},{17,25},{10,2},{2,... | collective-permute-start | bytes 49160 | tf_op jit(solution)/shard_map/ppermute | solution.py:48
  (68 shorter events, 26.4 us)
Async XLA Ops:
  1.6 9.1 %collective-permute-start.3 = (f32[32,128]{1,0:T(8,128)S(1)}, f32[32,128]{1,0:T(8,128)S(1)}, u32[]{:S(2)}, u32[]{:S(2)}) collective-permute-start(f32[32,128]{1,0:T(8,128)S(1)} %get-tuple-element.37), channel_id=1, source_target_pairs={{8,0},{0,8},{24,16},{16,24},{9,1},{1,9},{25,17},{17,25},{10,2},{2,... | collective-permute-start | bytes 49160 | tf_op jit(solution)/shard_map/ppermute | solution.py:48
  4.6 8.5 %collective-permute-start.4 = (f32[32,128]{1,0:T(8,128)S(1)}, f32[32,128]{1,0:T(8,128)S(1)}, u32[]{:S(2)}, u32[]{:S(2)}) collective-permute-start(f32[32,128]{1,0:T(8,128)S(1)} %get-tuple-element.38), channel_id=1, source_target_pairs={{16,0},{24,8},{0,16},{8,24},{17,1},{25,9},{1,17},{9,25},{18,2},{26... | collective-permute-start | bytes 49160 | tf_op jit(solution)/shard_map/ppermute | solution.py:48
  6.1 7.5 %collective-permute-start.5 = (f32[32,128]{1,0:T(8,128)S(1)}, f32[32,128]{1,0:T(8,128)S(1)}, u32[]{:S(2)}, u32[]{:S(2)}) collective-permute-start(f32[32,128]{1,0:T(8,128)S(1)} %get-tuple-element.39), channel_id=1, source_target_pairs={{24,0},{16,8},{8,16},{0,24},{25,1},{17,9},{9,17},{1,25},{26,2},{18... | collective-permute-start | bytes 49160 | tf_op jit(solution)/shard_map/ppermute | solution.py:48
  6.1 9.0 %collective-permute-start.11 = (f32[128,512]{1,0:T(8,128)}, f32[128,512]{1,0:T(8,128)S(1)}, u32[]{:S(2)}, u32[]{:S(2)}) collective-permute-start(f32[128,512]{1,0:T(8,128)} %refs_0_), channel_id=1, source_target_pairs={{0,2},{1,3},{2,0},{3,1},{4,6},{5,7},{6,4},{7,5},{8,10},{9,11},{10,... | collective-permute-start | bytes 786440 | tf_op jit(solution)/shard_map/ppermute | solution.py:40
  8.2 13.6 %collective-permute-start.6 = (f32[128,512]{1,0:T(8,128)}, f32[128,512]{1,0:T(8,128)S(1)}, u32[]{:S(2)}, u32[]{:S(2)}) collective-permute-start(f32[128,512]{1,0:T(8,128)} %refs_0_), channel_id=1, source_target_pairs={{0,6},{1,7},{2,4},{3,5},{4,2},{5,3},{6,0},{7,1},{8,14},{9,15},{10,... | collective-permute-start | bytes 786440 | tf_op jit(solution)/shard_map/ppermute | solution.py:40
  10.7 12.6 %collective-permute-start.2 = (f32[128,512]{1,0:T(8,128)}, f32[128,512]{1,0:T(8,128)S(1)}, u32[]{:S(2)}, u32[]{:S(2)}) collective-permute-start(f32[128,512]{1,0:T(8,128)} %refs_0_), channel_id=1, source_target_pairs={{24,0},{16,8},{8,16},{0,24},{25,1},{17,9},{9,17},{1,25},{26,2},{18... | collective-permute-start | bytes 786440 | tf_op jit(solution)/shard_map/ppermute | solution.py:48
  13.1 11.4 %collective-permute-start.1 = (f32[128,512]{1,0:T(8,128)}, f32[128,512]{1,0:T(8,128)S(1)}, u32[]{:S(2)}, u32[]{:S(2)}) collective-permute-start(f32[128,512]{1,0:T(8,128)} %refs_0_), channel_id=1, source_target_pairs={{16,0},{24,8},{0,16},{8,24},{17,1},{25,9},{1,17},{9,25},{18,2},{26... | collective-permute-start | bytes 786440 | tf_op jit(solution)/shard_map/ppermute | solution.py:48
  13.6 10.9 %collective-permute-start = (f32[128,512]{1,0:T(8,128)}, f32[128,512]{1,0:T(8,128)S(1)}, u32[]{:S(2)}, u32[]{:S(2)}) collective-permute-start(f32[128,512]{1,0:T(8,128)} %refs_0_), channel_id=1, source_target_pairs={{8,0},{0,8},{24,16},{16,24},{9,1},{1,9},{25,17},{17,25},{10,2},{2,... | collective-permute-start | bytes 786440 | tf_op jit(solution)/shard_map/ppermute | solution.py:48
  15.2 15.0 %collective-permute-start.13 = (f32[128,512]{1,0:T(8,128)S(1)}, f32[128,512]{1,0:T(8,128)S(1)}, u32[]{:S(2)}, u32[]{:S(2)}) collective-permute-start(f32[128,512]{1,0:T(8,128)S(1)} %collective-permute-done.11.refs_2_), channel_id=1, source_target_pairs={{16,0},{24,8},{0,16},{8,24},{17,1},{25,9},{1,17},{9,25},{18,2},{26... | collective-permute-start | bytes 786440 | tf_op jit(solution)/shard_map/ppermute | solution.py:48
  21.8 13.5 %collective-permute-start.8 = (f32[128,512]{1,0:T(8,128)S(1)}, f32[128,512]{1,0:T(8,128)S(1)}, u32[]{:S(2)}, u32[]{:S(2)}) collective-permute-start(f32[128,512]{1,0:T(8,128)S(1)} %collective-permute-done.6.refs_2_), channel_id=1, source_target_pairs={{16,0},{24,8},{0,16},{8,24},{17,1},{25,9},{1,17},{9,25},{18,2},{26... | collective-permute-start | bytes 786440 | tf_op jit(solution)/shard_map/ppermute | solution.py:48
  27.4 23.3 %collective-permute-start.16 = (f32[512,512]{1,0:T(8,128)S(1)}, f32[512,512]{1,0:T(8,128)S(1)}, u32[]{:S(2)}, u32[]{:S(2)}) collective-permute-start(f32[512,512]{1,0:T(8,128)S(1)} %get-tuple-element.46), channel_id=1, source_target_pairs={{1,0},{0,1},{3,2},{2,3},{5,4},{4,5},{7,6},{6,7},{9,8},{8,9},{11,10... | collective-permute-start | bytes 3145736 | tf_op jit(solution)/shard_map/ppermute | solution.py:44
  27.5 9.4 %collective-permute-start.12 = (f32[128,512]{1,0:T(8,128)S(1)}, f32[128,512]{1,0:T(8,128)S(1)}, u32[]{:S(2)}, u32[]{:S(2)}) collective-permute-start(f32[128,512]{1,0:T(8,128)S(1)} %collective-permute-done.11.refs_2_), channel_id=1, source_target_pairs={{8,0},{0,8},{24,16},{16,24},{9,1},{1,9},{25,17},{17,25},{10,2},{2,... | collective-permute-start | bytes 786440 | tf_op jit(solution)/shard_map/ppermute | solution.py:48
  28.6 13.2 %collective-permute-start.7 = (f32[128,512]{1,0:T(8,128)S(1)}, f32[128,512]{1,0:T(8,128)S(1)}, u32[]{:S(2)}, u32[]{:S(2)}) collective-permute-start(f32[128,512]{1,0:T(8,128)S(1)} %collective-permute-done.6.refs_2_), channel_id=1, source_target_pairs={{8,0},{0,8},{24,16},{16,24},{9,1},{1,9},{25,17},{17,25},{10,2},{2,... | collective-permute-start | bytes 786440 | tf_op jit(solution)/shard_map/ppermute | solution.py:48
  30.2 12.3 %collective-permute-start.14 = (f32[128,512]{1,0:T(8,128)S(1)}, f32[128,512]{1,0:T(8,128)S(1)}, u32[]{:S(2)}, u32[]{:S(2)}) collective-permute-start(f32[128,512]{1,0:T(8,128)S(1)} %collective-permute-done.2.refs_3_), channel_id=1, source_target_pairs={{0,2},{1,3},{2,0},{3,1},{4,6},{5,7},{6,4},{7,5},{8,10},{9,11},{10,... | collective-permute-start | bytes 786440 | tf_op jit(solution)/shard_map/ppermute | solution.py:40
  35.3 10.3 %collective-permute-start.9 = (f32[128,512]{1,0:T(8,128)S(1)}, f32[128,512]{1,0:T(8,128)S(1)}, u32[]{:S(2)}, u32[]{:S(2)}) collective-permute-start(f32[128,512]{1,0:T(8,128)S(1)} %collective-permute-done.2.refs_3_), channel_id=1, source_target_pairs={{0,6},{1,7},{2,4},{3,5},{4,2},{5,3},{6,0},{7,1},{8,14},{9,15},{10,... | collective-permute-start | bytes 786440 | tf_op jit(solution)/shard_map/ppermute | solution.py:40
  36.8 8.8 %collective-permute-start.17 = (f32[32,512]{1,0:T(8,128)S(1)}, f32[32,512]{1,0:T(8,128)S(1)}, u32[]{:S(2)}, u32[]{:S(2)}) collective-permute-start(f32[32,512]{1,0:T(8,128)S(1)} %shard_map.42.refs_4_.refs_15_), channel_id=1, source_target_pairs={{1,0},{0,1},{3,2},{2,3},{5,4},{4,5},{7,6},{6,7},{9,8},{8,9},{11,10... | collective-permute-start | bytes 196616 | tf_op jit(solution)/shard_map/ppermute | solution.py:44
  42.5 6.2 %collective-permute-start.10 = (f32[32,512]{1,0:T(8,128)S(1)}, f32[32,512]{1,0:T(8,128)S(1)}, u32[]{:S(2)}, u32[]{:S(2)}) collective-permute-start(f32[32,512]{1,0:T(8,128)S(1)} %shard_map.42.refs_4_.refs_15_), channel_id=1, source_target_pairs={{0,6},{1,7},{2,4},{3,5},{4,2},{5,3},{6,0},{7,1},{8,14},{9,15},{10,... | collective-permute-start | bytes 196616 | tf_op jit(solution)/shard_map/ppermute | solution.py:40
  45.6 9.3 %collective-permute-start.18 = (f32[128,512]{1,0:T(8,128)S(1)}, f32[128,512]{1,0:T(8,128)S(1)}, u32[]{:S(2)}, u32[]{:S(2)}) collective-permute-start(f32[128,512]{1,0:T(8,128)S(1)} %broadcast_select_fusion.3), channel_id=1, source_target_pairs={{1,0},{0,1},{3,2},{2,3},{5,4},{4,5},{7,6},{6,7},{9,8},{8,9},{11,10... | collective-permute-start | bytes 786440 | tf_op jit(solution)/shard_map/ppermute | solution.py:44
  45.7 9.2 %collective-permute-start.20 = (f32[128,512]{1,0:T(8,128)S(1)}, f32[128,512]{1,0:T(8,128)S(1)}, u32[]{:S(2)}, u32[]{:S(2)}) collective-permute-start(f32[128,512]{1,0:T(8,128)S(1)} %broadcast_select_fusion.1), channel_id=1, source_target_pairs={{1,0},{0,1},{3,2},{2,3},{5,4},{4,5},{7,6},{6,7},{9,8},{8,9},{11,10... | collective-permute-start | bytes 786440 | tf_op jit(solution)/shard_map/ppermute | solution.py:44
  46.4 8.5 %collective-permute-start.19 = (f32[128,512]{1,0:T(8,128)S(1)}, f32[128,512]{1,0:T(8,128)S(1)}, u32[]{:S(2)}, u32[]{:S(2)}) collective-permute-start(f32[128,512]{1,0:T(8,128)S(1)} %broadcast_select_fusion.2), channel_id=1, source_target_pairs={{1,0},{0,1},{3,2},{2,3},{5,4},{4,5},{7,6},{6,7},{9,8},{8,9},{11,10... | collective-permute-start | bytes 786440 | tf_op jit(solution)/shard_map/ppermute | solution.py:44
  48.7 6.2 %collective-permute-start.21 = (f32[128,512]{1,0:T(8,128)S(1)}, f32[128,512]{1,0:T(8,128)S(1)}, u32[]{:S(2)}, u32[]{:S(2)}) collective-permute-start(f32[128,512]{1,0:T(8,128)S(1)} %broadcast_select_fusion), channel_id=1, source_target_pairs={{1,0},{0,1},{3,2},{2,3},{5,4},{4,5},{7,6},{6,7},{9,8},{8,9},{11,10... | collective-permute-start | bytes 786440 | tf_op jit(solution)/shard_map/ppermute | solution.py:44
  57.1 6.5 %collective-permute-start.24 = (f32[40,512]{1,0:T(8,128)S(1)}, f32[40,512]{1,0:T(8,128)S(1)}, u32[]{:S(2)}, u32[]{:S(2)}) collective-permute-start(f32[40,512]{1,0:T(8,128)S(1)} %get-tuple-element.62.refs_10_.refs_16_), channel_id=1, source_target_pairs={{0,2},{1,3},{2,0},{3,1},{4,6},{5,7},{6,4},{7,5},{8,10},{9,11},{10,... | collective-permute-start | bytes 245768 | tf_op jit(solution)/shard_map/ppermute | solution.py:40
  60.5 6.3 %collective-permute-start.23 = (f32[40,512]{1,0:T(8,128)S(1)}, f32[40,512]{1,0:T(8,128)S(1)}, u32[]{:S(2)}, u32[]{:S(2)}) collective-permute-start(f32[40,512]{1,0:T(8,128)S(1)} %get-tuple-element.62.refs_10_.refs_16_), channel_id=1, source_target_pairs={{0,6},{1,7},{2,4},{3,5},{4,2},{5,3},{6,0},{7,1},{8,14},{9,15},{10,... | collective-permute-start | bytes 245768 | tf_op jit(solution)/shard_map/ppermute | solution.py:40
  69.8 6.7 %collective-permute-start.27 = (f32[40,512]{1,0:T(8,128)S(1)}, f32[40,512]{1,0:T(8,128)S(1)}, u32[]{:S(2)}, u32[]{:S(2)}) collective-permute-start(f32[40,512]{1,0:T(8,128)S(1)} %shard_map.48.refs_10_.refs_17_), channel_id=1, source_target_pairs={{0,6},{1,7},{2,4},{3,5},{4,2},{5,3},{6,0},{7,1},{8,14},{9,15},{10,... | collective-permute-start | bytes 245768 | tf_op jit(solution)/shard_map/ppermute | solution.py:40
  (12 other events, 40.7 us)

commit v2 on v1

--- a/solution.py
+++ b/solution.py
@@ -16,7 +16,8 @@
     -32.0 / (15.0 * math.pi) - 192.0 / (35.0 * math.pi),
     128.0 / (35.0 * math.pi),
 )
-EXTRA_ROWS = 8
+SUBLANES = 8
+LANES = 128
 VMEM = pl.BlockSpec(memory_space=pltpu.VMEM)
 ANY = pl.BlockSpec(memory_space=pl.ANY)
 NN = (((1,), (0,)), ((), ()))
@@ -44,6 +45,10 @@
     return lax.ppermute(block, "col", [(i ^ 1, i) for i in range(lax.axis_size("col"))])
 
 
+def chip_xor(block, mask):
+    return lax.ppermute(block, "col", [(i ^ (2 * mask), i) for i in range(lax.axis_size("col"))])
+
+
 def row_xor(block, mask):
     return lax.ppermute(block, "row", [(i ^ mask, i) for i in range(lax.axis_size("row"))])
 
@@ -62,10 +67,9 @@
     return lax.dot_general(a, b, dims, preferred_element_type=jnp.float32)
 
 
-def normalize(pieces):
-    members = sum(p.shape[0] for p in pieces)
-    x = jnp.concatenate([p[...] for p in pieces], 0)
-    centered = x - jnp.sum(x, 0, keepdims=True) / members
+def normalize(pieces, quarter):
+    x = jnp.concatenate([p[:quarter, :] for p in pieces], 0)
+    centered = x - jnp.sum(x, 0, keepdims=True) / x.shape[0]
     spread = jnp.sqrt(jnp.sum(centered * centered, 0, keepdims=True) + EPSILON)
     return centered * (1.0 / spread)
 
@@ -74,20 +78,21 @@
     return lax.axis_index("col") & 1
 
 
-def gram_kernel(window, count, offset, raw, last, *refs):
+def gram_kernel(window, count, members, probes, offset, raw, last, explicit, *refs):
     refs = list(refs)
     take = lambda k: [refs.pop(0) for _ in range(k)]
     own = offset is None
     left_high_ref, left_low_ref = (None, None) if own else take(2)
     pieces = take(count)
-    (w_ref,) = take(1)
+    w_ref = take(1)[0] if explicit else pieces[-1].at[pl.ds(members // count, probes), :]
     sum_ref, squares_ref = (None, None) if own else take(2)
     high_ref, low_ref, y_ref, square_ref = take(4)
-    normed = normalize(pieces) if raw else pieces[0][...]
+    normed = normalize(pieces, members // count) if raw else pieces[0][:members, :]
     n = normed.shape[1]
     if own:
         left_high_out, left_low_out, normed_out = take(3)
-        normed_out[...] = normed
+        normed_out[:members, :] = normed
+        normed_out[members:, :] = w_ref[...]
         left_high, left_low = split(normed.T)
         left_high_out[...] = left_high
         left_low_out[...] = left_low
@@ -102,50 +107,46 @@
     high, low = split(tapered)
     high_ref[...] = high
     low_ref[...] = low
-    square = jnp.sum((tapered * tapered).reshape(n // 8, 8, n), 0)
-    product = band_product([(high_ref, low_ref)], [w_ref], w_ref.shape[0])
+    square = jnp.sum((tapered * tapered).reshape(n // SUBLANES, SUBLANES, n), 0)
+    product = band_product([(high_ref, low_ref)], [w_ref])
     if not own:
         square += squares_ref[...]
         product += sum_ref[...]
-    probes = product.shape[0]
-    y_ref[:probes, :] = product
+    y_ref[...] = product
     if last:
-        total = jnp.sum(jnp.sum(square, 1, keepdims=True), 0, keepdims=True)
-        y_ref[probes:, :] = jnp.broadcast_to(total, (EXTRA_ROWS, n))
+        square = functools.reduce(jnp.add, [square[:, k : k + LANES] for k in range(0, n, LANES)])
     square_ref[...] = square
 
 
-def gram(offset, left, pieces, w, carried, window, raw=True, last=False):
+def gram(offset, left, pieces, w, shape, carried, window, raw=True, last=False):
     own = offset is None
-    n = pieces[0].shape[1]
-    members = sum(p.shape[0] for p in pieces)
-    probes = w.shape[0]
+    members, probes, n = shape
+    behind = [] if w is None else [w]
     band = jax.ShapeDtypeStruct((n, n), jnp.bfloat16)
     side = jax.ShapeDtypeStruct((n, members), jnp.bfloat16)
-    y = jax.ShapeDtypeStruct((probes + (EXTRA_ROWS if last else 0), n), jnp.float32)
-    outs = [band, band, y, jax.ShapeDtypeStruct((8, n), jnp.float32)]
-    operands = [*pieces, w]
+    square = jax.ShapeDtypeStruct((SUBLANES, LANES if last else n), jnp.float32)
+    outs = [band, band, jax.ShapeDtypeStruct((probes, n), jnp.float32), square]
     if own:
-        outs += [side, side, jax.ShapeDtypeStruct((members, n), jnp.float32)]
+        operands = [*pieces, *behind]
+        outs += [side, side, jax.ShapeDtypeStruct((members + probes, n), jnp.float32)]
     else:
-        operands = [*left, *operands, *carried]
-    specs = [VMEM] * len(operands)
+        operands = [*left, *pieces, *behind, *carried]
     return pl.pallas_call(
-        functools.partial(gram_kernel, window, len(pieces), offset, raw, last),
+        functools.partial(gram_kernel, window, len(pieces), members, probes, offset, raw, last, w is not None),
         out_shape=tuple(outs),
         compiler_params=vmem_limit(*operands, *outs, scratch=16 * n * (n + members)),
-        in_specs=specs,
+        in_specs=[VMEM] * len(operands),
         out_specs=[VMEM] * len(outs),
         cost_estimate=pl.CostEstimate(flops=6 * n * n * members, bytes_accessed=4 * n * members, transcendentals=0),
     )(*operands)
 
 
-def band_product(bands, windows, probes):
-    n = bands[0][0].shape[0]
+def band_product(bands, windows):
+    probes, n = windows[0].shape
     wide = jnp.zeros((2 * probes, n), jnp.float32)
     narrow = jnp.zeros((probes, n), jnp.float32)
     for (high_ref, low_ref), w_ref in zip(bands, windows):
-        high, low = split(w_ref[:probes, :])
+        high, low = split(w_ref[...])
         band_high = high_ref[...]
         wide += dot(jnp.concatenate([high, low], 0), band_high, NT)
         narrow += dot(high, low_ref[...], NT)
@@ -157,38 +158,22 @@
     return bands, refs[2 * slots : 3 * slots], refs[3 * slots :]
 
 
-def second_kernel(slots, probes, reach_pairs, *refs):
-    bands, windows, (y_ref,) = unpack(refs, slots)
-    y_ref[:probes, :] = band_product(bands, windows, probes)
-    here = [windows[k][probes : probes + 1, :] for k in range(2 * reach_pairs + 1)]
-    ahead = jnp.zeros_like(here[0])
-    behind = jnp.zeros_like(here[0])
-    for span in range(1, reach_pairs + 1):
-        first, second = here[2 * span - 1], here[2 * span]
-        flag = side_sign((span, 0)) > 0
-        ahead += jnp.where(flag, first, second)
-        if span < reach_pairs:
-            behind += jnp.where(flag, second, first)
-    y_ref[probes : probes + 1, :] = functools.reduce(jnp.add, here)
-    y_ref[probes + 1 : probes + 2, :] = ahead
-    y_ref[probes + 2 : probes + 3, :] = behind
-    y_ref[probes + 3 :, :] = jnp.zeros((EXTRA_ROWS - 3, y_ref.shape[1]), jnp.float32)
-
-
-def last_kernel(slots, probes, reach_pairs, state_count, *refs):
-    bands, windows, (w0_ref, y1_ref, y2_ref, *out_refs, total_ref) = unpack(refs, slots)
-    y3 = band_product(bands, windows, probes)
-    first, second = windows[2 * reach_pairs - 1], windows[2 * reach_pairs]
-    flag = side_sign((reach_pairs, 0)) > 0
-    sums = y2_ref[probes : probes + 1, :]
-    sums += jnp.where(flag, first[probes + 1 : probes + 2, :], second[probes + 1 : probes + 2, :])
-    sums += jnp.where(flag, second[probes + 2 : probes + 3, :], first[probes + 2 : probes + 3, :])
-    for row in range(probes, probes + 3):
-        sums += windows[-1][row : row + 1, :]
-    scale = sums / state_count
+def step_kernel(slots, follows, *refs):
+    bands, windows, rest = unpack(refs, slots)
+    product = band_product(bands, windows)
+    if follows:
+        product += rest[0][...]
+    rest[-1][...] = product
+
+
+def last_kernel(slots, state_count, *refs):
+    bands, windows, (sum_ref, square_ref, w0_ref, y1_ref, y2_ref, *out_refs, total_ref) = unpack(refs, slots)
+    y3 = band_product(bands, windows) + sum_ref[...]
+    squares = jnp.sum(jnp.sum(square_ref[...], 1, keepdims=True), 0, keepdims=True)
+    scale = jnp.broadcast_to(squares, (1, y3.shape[1])) / state_count
     total = POWER_TERMS[0] * w0_ref[...]
-    total += POWER_TERMS[1] * (y1_ref[:probes, :] / scale)
-    total += POWER_TERMS[2] * (y2_ref[:probes, :] / scale / scale)
+    total += POWER_TERMS[1] * (y1_ref[...] / scale)
+    total += POWER_TERMS[2] * (y2_ref[...] / scale / scale)
     total += POWER_TERMS[3] * (y3 / scale / scale / scale)
     total_ref[...] = jnp.sqrt(scale) * total
     width = out_refs[0].shape[1]
@@ -227,7 +212,7 @@
     return pl.pallas_call(
         kernel,
         out_shape=outs,
-        compiler_params=vmem_limit(*operands, *operands),
+        compiler_params=vmem_limit(*operands, *jax.tree.leaves(outs)),
         in_specs=[VMEM] * len(operands),
         out_specs=jax.tree.map(lambda _: VMEM, outs),
         scratch_shapes=scratch,
@@ -313,20 +298,26 @@
     keys = [None] + [(span, late) for span in range(1, pairs + 1) for late in (0, 1)]
     inner_keys = keys[: 2 * pairs - 1]
     last_pair = keys[-2:]
-
-    def window_of(held, outer):
-        inner = [core_swap(held[k]) for k in inner_keys]
-        return [held[k] for k in keys] + inner + [core_swap(outer)]
-
-    first_ahead = side_sign(last_pair[0]) > 0
-    far_first = first_ahead == (device_core() == 0)
-    perturbations, first_ahead, far_first = lax.optimization_barrier((perturbations, first_ahead, far_first))
+    far_first = (side_sign(last_pair[0]) > 0) == (device_core() == 0)
+    perturbations, far_first = lax.optimization_barrier((perturbations, far_first))
 
     def far_pick(held):
         return jnp.where(far_first, held[last_pair[0]], held[last_pair[1]])
 
     def exchange(block):
-        return {None: block} | {k: ring_swap(block, k) for k in sides}
+        held = {None: block} | {k: ring_swap(block, k) for k in sides}
+        inner = [core_swap(held[k]) for k in inner_keys]
+        return [held[k] for k in keys] + inner + [core_swap(far_pick(held))]
+
+    piece = jax.ShapeDtypeStruct((probe_count, n // row_count), jnp.float32)
+    quarter = perturbations.shape[0]
+    members = quarter * row_count
+    shape = (members, probe_count, n)
+    turned = pltpu.VMEM((probes.shape[1], probes.shape[0]), jnp.float32)
+    shares = small_call(split_kernel, [probes], [piece] * row_count, [turned])
+    shares = [shares[0]] + [row_xor(shares[mask], mask) for mask in range(1, row_count)]
+    w0 = small_call(join_kernel, shares, jax.ShapeDtypeStruct((probe_count, n), jnp.float32))
+    w_side = {None: w0} | {k: ring_swap(w0, k) for k in sides}
 
     last_mask = row_count - 1
     blocks = {None: {0: perturbations}}
@@ -334,13 +325,7 @@
         blocks[k] = {0: ring_swap(perturbations, k)}
     for mask in range(last_mask, 0, -1):
         blocks[None][mask] = row_xor(perturbations, mask)
-    piece = jax.ShapeDtypeStruct((probe_count, n // row_count), jnp.float32)
-    turned = pltpu.VMEM((probes.shape[1], probes.shape[0]), jnp.float32)
-    pieces = small_call(split_kernel, [probes], [piece] * row_count, [turned])
-    pieces = [pieces[0]] + [row_xor(pieces[mask], mask) for mask in range(1, row_count)]
-    w0 = small_call(join_kernel, pieces, jax.ShapeDtypeStruct((probe_count, n), jnp.float32))
-    held = exchange(w0)
-    windows = window_of(held, far_pick(held))
+    blocks[None] = dict(sorted(blocks[None].items()))
     for k in sides:
         for mask in range(1, last_mask):
             blocks[k][mask] = row_xor(blocks[k][0], mask)
@@ -357,49 +342,62 @@
     offsets.append(lambda: (1 - reach) * (1 - 2 * device_core()))
     slots = len(offsets)
     bands = {}
-    own_pieces = [blocks[None][mask] for mask in range(row_count)]
-    high, low, y1, square, *left, normed = gram(None, None, own_pieces, windows[0], None, window)
+    own_pieces = list(blocks[None].values())
+    high, low, y1, square, *left, normed = gram(None, None, own_pieces, w0, shape, None, window)
     bands[0] = (high, low)
 
-    def add_slot(k, pieces, carried, **kinds):
-        high, low, *carried = gram(offsets[k], left, pieces, windows[k], carried, window, **kinds)
+    def add_slot(k, pieces, w, carried, **kinds):
+        high, low, *carried = gram(offsets[k], left, pieces, w, shape, carried, window, **kinds)
         bands[k] = (high, low)
         return carried
 
     def add_side(k, carried):
-        return add_slot(keys.index(k), list(blocks[k].values()), carried)
+        return add_slot(keys.index(k), list(blocks[k].values()), w_side[k], carried)
 
     carried = [y1, square]
     near_block = core_swap(normed)
-    far = [core_swap(far_pick({k: blocks[k][mask] for k in sides})) for mask in range(row_count)]
-    for k in sides[:pairs]:
+    far = [far_pick({k: blocks[k][mask] for k in sides}) for mask in range(row_count)]
+    far[-1] = jnp.concatenate([far[-1], far_pick(w_side)], 0)
+    far = [core_swap(block) for block in far]
+    carried = add_slot(len(keys), [near_block], None, carried, raw=False)
+    for k in sides:
         carried = add_side(k, carried)
-    for place, k in enumerate(inner_keys):
-        slot = len(keys) + place
-        if k is None:
-            carried = add_slot(slot, [near_block], carried, raw=False)
-        else:
-            pieces = [core_swap(block) for block in blocks[k].values()]
-            carried = add_slot(slot, pieces, carried)
-    for k in sides[pairs:]:
-        carried = add_side(k, carried)
-    y1, _ = add_slot(slots - 1, far, carried, last=True)
+    for place, k in enumerate(inner_keys[1:], 1):
+        pieces = [core_swap(block) for block in blocks[k].values()]
+        w = core_swap(w_side[k])
+        carried = add_slot(len(keys) + place, pieces, w, carried)
+    y1, squares = add_slot(slots - 1, far, None, carried, last=True)
     bands = [bands[k] for k in range(slots)]
 
     localized = skewed(offsets, reach, bands)
 
-    held = exchange(y1)
-    windows = window_of(held, far_pick(held))
-    second = functools.partial(second_kernel, slots, probe_count, pairs)
-    y2 = step_call(second, bands, windows, [], jax.ShapeDtypeStruct(y1.shape, y1.dtype))
-    held = exchange(y2)
-    row = lax.broadcasted_iota(jnp.int32, y2.shape, 0) - probe_count
-    first, second = held[last_pair[0]], held[last_pair[1]]
-    tail = jnp.where(row == 0, y2, jnp.where((row == 1) == first_ahead, first, second))
-    windows = window_of(held, jnp.where(row < 0, far_pick(held), tail))
+
+    squares += core_swap(squares)
+    mask = 1
+    while mask < col_count // 2:
+        squares += chip_xor(squares, mask)
+        mask *= 2
+
+    near = [0, len(keys)]
+    beside = list(range(1, len(keys)))
+    rest = list(range(len(keys) + 1, slots))
+
+    def advance(block):
+        windows = exchange(block)
+        pick = lambda items, places: [items[k] for k in places]
+        shape = jax.ShapeDtypeStruct(block.shape, block.dtype)
+        first = functools.partial(step_kernel, len(near), False)
+        total = step_call(first, pick(bands, near), pick(windows, near), [], shape)
+        second = functools.partial(step_kernel, len(beside), True)
+        total = step_call(second, pick(bands, beside), pick(windows, beside), [total], shape)
+        return pick(bands, rest), pick(windows, rest), [total], shape
+
+    *parts, shape = advance(y1)
+    y2 = step_call(functools.partial(step_kernel, len(rest), True), *parts, shape)
+    far_bands, far_windows, total, shape = advance(y2)
     pieces = step_call(
-        functools.partial(last_kernel, slots, probe_count, pairs, state_count),
-        bands, windows, [w0, y1, y2], [piece] * row_count,
+        functools.partial(last_kernel, len(rest), state_count),
+        far_bands, far_windows, total + [squares, w0, y1, y2], [piece] * row_count,
         scratch=[pltpu.VMEM((probe_count, n), jnp.float32)],
     )
     pieces = [pieces[0]] + [row_xor(pieces[mask], mask) for mask in range(1, row_count)]

time: 87.3 us -> 96.2 us (1.10)
  waiting for transfers between devices: 34.8 us -> 45.2 us
  starting transfers between devices: 34.2 us -> 32.5 us
    ppermute x0 -> x2, waiting for transfers between devices: none -> 7.37 us  [chip_xor(): lax.ppermute(block, 'col', [(i ^ 2 * mask, i) for i in range(lax.axis_siz...]
    ppermute x10, waiting for transfers between devices: 19.4 us -> 22.3 us  [ring_swap(): return lax.ppermute(block, 'col', route)]
    ppermute x13, starting transfers between devices: 16.7 us -> 14.3 us  [row_xor(): lax.ppermute(block, 'row', [(i ^ mask, i) for i in range(lax.axis_size('r...]
    ppermute x13, waiting for transfers between devices: 12.8 us -> 14.7 us  [row_xor(): lax.ppermute(block, 'row', [(i ^ mask, i) for i in range(lax.axis_size('r...]
    ppermute x11 -> x10, waiting for transfers between devices: 2.58 us -> 0.91 us  [core_swap(): lax.ppermute(block, 'col', [(i ^ 1, i) for i in range(lax.axis_size('col'...]
    pallas_call x2 -> x6, Pallas kernels: 3.3 us -> 3.72 us  [step_call(): pl.pallas_call(kernel, out_shape=outs, compiler_params=vmem_limit(*operan...]
  transfers between devices with their start and end apart: 34 -> 35, of which waited for: 17 -> 20; matrix products, arithmetic and copies ran while one was open for 0% -> 0% of each run, Pallas kernels for 10% -> 12%
where the time goes in v2:
time: 96.2 us; the launch traced here: 96 us
  waiting for transfers between devices  45.2 us (47%)
  starting transfers between devices  32.5 us (34%)
  Pallas kernels  15.4 us (16%)
  local copies, waits for them, and re-layouts  1.78 us (2%)
    ppermute x10, waiting for transfers between devices, ring_swap(): return lax.ppermute(block, 'col', route)  22.3 us
    ppermute x10, starting transfers between devices, ring_swap(): return lax.ppermute(block, 'col', route)  16.3 us
    ppermute x13, waiting for transfers between devices, row_xor(): lax.ppermute(block, 'row', [(i ^ mask, i) for i in range(lax.axis_size('r...  14.7 us
    ppermute x13, starting transfers between devices, row_xor(): lax.ppermute(block, 'row', [(i ^ mask, i) for i in range(lax.axis_size('r...  14.3 us
    pallas_call x5, Pallas kernels, gram(): pl.pallas_call(functools.partial(gram_kernel, window, len(pieces), member...  9.31 us
    ppermute x2, waiting for transfers between devices, chip_xor(): lax.ppermute(block, 'col', [(i ^ 2 * mask, i) for i in range(lax.axis_siz...  7.37 us
    pallas_call x6, Pallas kernels, step_call(): pl.pallas_call(kernel, out_shape=outs, compiler_params=vmem_limit(*operan...  3.72 us
  transfers between devices with their start and end apart: 35, of which 20 were waited for; matrix products, arithmetic and copies ran while one was open for 0% of the time, Pallas kernels for 12%

profile of v2, /device:TPU:0, one launch (start us, length us, event | category | flops | bytes accessed | tf_op | source)
XLA Modules:
  0.0 96.0 jit_solution(13148275589568797818)
XLA Ops:
  1.6 3.0 %collective-permute-start.3 = (f32[32,128]{1,0:T(8,128)S(1)}, f32[32,128]{1,0:T(8,128)S(1)}, u32[]{:S(2)}, u32[]{:S(2)}) collective-permute-start(f32[32,128]{1,0:T(8,128)S(1)} %get-tuple-element.37), channel_id=1, source_target_pairs={{8,0},{0,8},{24,16},{16,24},{9,1},{1,9},{25,17},{17,25},{10,2},{2,... | collective-permute-start | bytes 49160 | tf_op jit(solution)/shard_map/ppermute | solution.py:53
  6.3 2.0 %collective-permute-done.4.refs_2_ = f32[32,128]{1,0:T(8,128)S(1)} collective-permute-done((f32[32,128]{1,0:T(8,128)S(1)}, f32[32,128]{1,0:T(8,128)S(1)}, u32[]{:S(2)}, u32[]{:S(2)}) %collective-permute-start.4) | collective-permute-done | bytes 16416 | tf_op jit(solution)/shard_map/ppermute | solution.py:53
  8.3 2.4 %collective-permute-done.5.refs_3_ = f32[32,128]{1,0:T(8,128)S(1)} collective-permute-done((f32[32,128]{1,0:T(8,128)S(1)}, f32[32,128]{1,0:T(8,128)S(1)}, u32[]{:S(2)}, u32[]{:S(2)}) %collective-permute-start.5) | collective-permute-done | bytes 16416 | tf_op jit(solution)/shard_map/ppermute | solution.py:53
  10.8 1.6 %collective-permute-start.16 = (f32[32,512]{1,0:T(8,128)S(1)}, f32[32,512]{1,0:T(8,128)S(1)}, u32[]{:S(2)}, u32[]{:S(2)}) collective-permute-start(f32[32,512]{1,0:T(8,128)S(1)} %shard_map.42.refs_4_.refs_5_), channel_id=1, source_target_pairs={{0,2},{1,3},{2,0},{3,1},{4,6},{5,7},{6,4},{7,5},{8,10},{9,11},{10,... | collective-permute-start | bytes 196616 | tf_op jit(solution)/shard_map/ppermute | solution.py:41
  12.4 2.5 %collective-permute-start.10 = (f32[32,512]{1,0:T(8,128)S(1)}, f32[32,512]{1,0:T(8,128)S(1)}, u32[]{:S(2)}, u32[]{:S(2)}) collective-permute-start(f32[32,512]{1,0:T(8,128)S(1)} %shard_map.42.refs_4_.refs_5_), channel_id=1, source_target_pairs={{0,6},{1,7},{2,4},{3,5},{4,2},{5,3},{6,0},{7,1},{8,14},{9,15},{10,... | collective-permute-start | bytes 196616 | tf_op jit(solution)/shard_map/ppermute | solution.py:41
  17.0 1.5 %collective-permute-start.1 = (f32[128,512]{1,0:T(8,128)}, f32[128,512]{1,0:T(8,128)S(1)}, u32[]{:S(2)}, u32[]{:S(2)}) collective-permute-start(f32[128,512]{1,0:T(8,128)} %refs_0_), channel_id=1, source_target_pairs={{16,0},{24,8},{0,16},{8,24},{17,1},{25,9},{1,17},{9,25},{18,2},{26... | collective-permute-start | bytes 786440 | tf_op jit(solution)/shard_map/ppermute | solution.py:53
  20.0 4.4 %collective-permute-done.12.refs_2_ = f32[128,512]{1,0:T(8,128)S(1)} collective-permute-done((f32[128,512]{1,0:T(8,128)}, f32[128,512]{1,0:T(8,128)S(1)}, u32[]{:S(2)}, u32[]{:S(2)}) %collective-permute-start.12) | collective-permute-done | bytes 262176 | tf_op jit(solution)/shard_map/ppermute | solution.py:41
  24.9 3.2 %collective-permute-done.6.refs_2_ = f32[128,512]{1,0:T(8,128)S(1)} collective-permute-done((f32[128,512]{1,0:T(8,128)}, f32[128,512]{1,0:T(8,128)S(1)}, u32[]{:S(2)}, u32[]{:S(2)}) %collective-permute-start.6) | collective-permute-done | bytes 262176 | tf_op jit(solution)/shard_map/ppermute | solution.py:41
  30.1 1.9 %shard_map.43 = (bf16[512,512]{1,0:T(8,128)(2,1)S(1)}, bf16[512,512]{1,0:T(8,128)(2,1)S(1)}, f32[32,512]{1,0:T(8,128)S(1)}, f32[8,512]{1,0:T(8,128)S(1)}, bf16[5...) custom-call(f32[128,512]{1,0:T(8,128)S(1)} %copy-done.1, ...), custom_call_target="tpu_custom_call" | custom-call | flops 805306368 | bytes 1048576 | tf_op jit(solution)/shard_map/pallas_call | solution.py:134
  33.1 2.4 %collective-permute-start.9 = (f32[128,512]{1,0:T(8,128)S(1)}, f32[128,512]{1,0:T(8,128)S(1)}, u32[]{:S(2)}, u32[]{:S(2)}) collective-permute-start(f32[128,512]{1,0:T(8,128)S(1)} %collective-permute-done.2.refs_3_), channel_id=1, source_target_pairs={{0,6},{1,7},{2,4},{3,5},{4,2},{5,3},{6,0},{7,1},{8,14},{9,15},{10,... | collective-permute-start | bytes 786440 | tf_op jit(solution)/shard_map/ppermute | solution.py:41
  35.6 3.6 %collective-permute-done.8.refs_4_ = f32[128,512]{1,0:T(8,128)S(1)} collective-permute-done((f32[128,512]{1,0:T(8,128)S(1)}, f32[128,512]{1,0:T(8,128)S(1)}, u32[]{:S(2)}, u32[]{:S(2)}) %collective-permute-start.8) | collective-permute-done | bytes 262176 | tf_op jit(solution)/shard_map/ppermute | solution.py:53
  42.0 5.8 %collective-permute-done.9.refs_5_ = f32[128,512]{1,0:T(8,128)S(1)} collective-permute-done((f32[128,512]{1,0:T(8,128)S(1)}, f32[128,512]{1,0:T(8,128)S(1)}, u32[]{:S(2)}, u32[]{:S(2)}) %collective-permute-start.9) | collective-permute-done | bytes 262176 | tf_op jit(solution)/shard_map/ppermute | solution.py:41
  48.5 3.5 %collective-permute-done.7.refs_3_ = f32[128,512]{1,0:T(8,128)S(1)} collective-permute-done((f32[128,512]{1,0:T(8,128)S(1)}, f32[128,512]{1,0:T(8,128)S(1)}, u32[]{:S(2)}, u32[]{:S(2)}) %collective-permute-start.7) | collective-permute-done | bytes 262176 | tf_op jit(solution)/shard_map/ppermute | solution.py:53
  52.2 1.6 %shard_map.44 = (bf16[512,512]{1,0:T(8,128)(2,1)S(1)}, bf16[512,512]{1,0:T(8,128)(2,1)S(1)}, f32[32,512]{1,0:T(8,128)S(1)}, f32[8,512]{1,0:T(8,128)S(1)}) custom-call(bf16[512,512]{1,0:T(8,128)(2,1)S(1)} %get-tuple-element.41.refs_0_, bf16[512,512]{1,0:T(8,128)(2,1)S(1)} %get-tuple-element.42.refs_1_, f32[544,512]{1,0:T(8,128)S(1)} %collective-permute-done.11.refs_2_, ...), custom_call_target="tpu_custom_call" | custom-call | flops 805306368 | bytes 1048576 | tf_op jit(solution)/shard_map/pallas_call | solution.py:134
  53.8 1.9 %shard_map.45 = (bf16[512,512]{1,0:T(8,128)(2,1)S(1)}, bf16[512,512]{1,0:T(8,128)(2,1)S(1)}, f32[32,512]{1,0:T(8,128)S(1)}, f32[8,512]{1,0:T(8,128)S(1)}) custom-call(bf16[512,512]{1,0:T(8,128)(2,1)S(1)} %get-tuple-element.41.refs_0_, bf16[512,512]{1,0:T(8,128)(2,1)S(1)} %get-tuple-element.42.refs_1_, f32[128,512]{1,0:T(8,128)S(1)} %collective-permute-done.6.refs_2_, ...), custom_call_target="tpu_custom_call" | custom-call | flops 805306368 | bytes 1048576 | tf_op jit(solution)/shard_map/pallas_call | solution.py:134
  55.7 1.9 %shard_map.46 = (bf16[512,512]{1,0:T(8,128)(2,1)S(1)}, bf16[512,512]{1,0:T(8,128)(2,1)S(1)}, f32[32,512]{1,0:T(8,128)S(1)}, f32[8,512]{1,0:T(8,128)S(1)}) custom-call(bf16[512,512]{1,0:T(8,128)(2,1)S(1)} %get-tuple-element.41.refs_0_, bf16[512,512]{1,0:T(8,128)(2,1)S(1)} %get-tuple-element.42.refs_1_, f32[128,512]{1,0:T(8,128)S(1)} %collective-permute-done.12.refs_2_, ...), custom_call_target="tpu_custom_call" | custom-call | flops 805306368 | bytes 1048576 | tf_op jit(solution)/shard_map/pallas_call | solution.py:134
  57.7 1.9 %shard_map.47 = (bf16[512,512]{1,0:T(8,128)(2,1)S(1)}, bf16[512,512]{1,0:T(8,128)(2,1)S(1)}, f32[32,512]{1,0:T(8,128)S(1)}, f32[8,128]{1,0:T(8,128)S(1)}) custom-call(bf16[512,512]{1,0:T(8,128)(2,1)S(1)} %get-tuple-element.41.refs_0_, bf16[512,512]{1,0:T(8,128)(2,1)S(1)} %get-tuple-element.42.refs_1_, f32[128,512]{1,0:T(8,128)S(1)} %collective-permute-done.17.refs_2_, ...), custom_call_target="tpu_custom_call" | custom-call | flops 805306368 | bytes 1048576 | tf_op jit(solution)/shard_map/pallas_call | solution.py:134
  60.0 3.4 %collective-permute-start.21 = (f32[32,512]{1,0:T(8,128)S(1)}, f32[32,512]{1,0:T(8,128)S(1)}, u32[]{:S(2)}, u32[]{:S(2)}) collective-permute-start(f32[32,512]{1,0:T(8,128)S(1)} %get-tuple-element.62.refs_4_.refs_6_), channel_id=1, source_target_pairs={{0,6},{1,7},{2,4},{3,5},{4,2},{5,3},{6,0},{7,1},{8,14},{9,15},{10,... | collective-permute-start | bytes 196616 | tf_op jit(solution)/shard_map/ppermute | solution.py:41
  64.2 3.4 %collective-permute-done.21.refs_4_ = f32[32,512]{1,0:T(8,128)S(1)} collective-permute-done((f32[32,512]{1,0:T(8,128)S(1)}, f32[32,512]{1,0:T(8,128)S(1)}, u32[]{:S(2)}, u32[]{:S(2)}) %collective-permute-start.21) | collective-permute-done | bytes 65568 | tf_op jit(solution)/shard_map/ppermute | solution.py:41
  70.3 2.6 %collective-permute-start.25 = (f32[32,512]{1,0:T(8,128)S(1)}, f32[32,512]{1,0:T(8,128)S(1)}, u32[]{:S(2)}, u32[]{:S(2)}) collective-permute-start(f32[32,512]{1,0:T(8,128)S(1)} %shard_map.50.refs_4_.refs_7_), channel_id=1, source_target_pairs={{0,6},{1,7},{2,4},{3,5},{4,2},{5,3},{6,0},{7,1},{8,14},{9,15},{10,... | collective-permute-start | bytes 196616 | tf_op jit(solution)/shard_map/ppermute | solution.py:41
  74.1 2.8 %collective-permute-done.25.refs_4_ = f32[32,512]{1,0:T(8,128)S(1)} collective-permute-done((f32[32,512]{1,0:T(8,128)S(1)}, f32[32,512]{1,0:T(8,128)S(1)}, u32[]{:S(2)}, u32[]{:S(2)}) %collective-permute-start.25) | collective-permute-done | bytes 65568 | tf_op jit(solution)/shard_map/ppermute | solution.py:41
  78.3 3.6 %collective-permute-done.30 = f32[8,128]{1,0:T(8,128)S(1)} collective-permute-done((f32[8,128]{1,0:T(8,128)S(1)}, f32[8,128]{1,0:T(8,128)S(1)}, u32[]{:S(2)}, u32[]{:S(2)}) %collective-permute-start.30) | collective-permute-done | bytes 4128 | tf_op jit(solution)/shard_map/ppermute | solution.py:49
  82.6 3.8 %collective-permute-done.31 = f32[8,128]{1,0:T(8,128)S(1)} collective-permute-done((f32[8,128]{1,0:T(8,128)S(1)}, f32[8,128]{1,0:T(8,128)S(1)}, u32[]{:S(2)}, u32[]{:S(2)}) %collective-permute-start.31) | collective-permute-done | bytes 4128 | tf_op jit(solution)/shard_map/ppermute | solution.py:49
  93.4 1.8 %collective-permute-done.34.refs_3_ = f32[32,128]{1,0:T(8,128)S(1)} collective-permute-done((f32[32,128]{1,0:T(8,128)S(1)}, f32[32,128]{1,0:T(8,128)S(1)}, u32[]{:S(2)}, u32[]{:S(2)}) %collective-permute-start.34) | collective-permute-done | bytes 16416 | tf_op jit(solution)/shard_map/ppermute | solution.py:53
  (76 shorter events, 28.3 us)
Async XLA Ops:
  1.6 4.8 %collective-permute-start.3 = (f32[32,128]{1,0:T(8,128)S(1)}, f32[32,128]{1,0:T(8,128)S(1)}, u32[]{:S(2)}, u32[]{:S(2)}) collective-permute-start(f32[32,128]{1,0:T(8,128)S(1)} %get-tuple-element.37), channel_id=1, source_target_pairs={{8,0},{0,8},{24,16},{16,24},{9,1},{1,9},{25,17},{17,25},{10,2},{2,... | collective-permute-start | bytes 49160 | tf_op jit(solution)/shard_map/ppermute | solution.py:53
  10.8 6.2 %collective-permute-start.16 = (f32[32,512]{1,0:T(8,128)S(1)}, f32[32,512]{1,0:T(8,128)S(1)}, u32[]{:S(2)}, u32[]{:S(2)}) collective-permute-start(f32[32,512]{1,0:T(8,128)S(1)} %shard_map.42.refs_4_.refs_5_), channel_id=1, source_target_pairs={{0,2},{1,3},{2,0},{3,1},{4,6},{5,7},{6,4},{7,5},{8,10},{9,11},{10,... | collective-permute-start | bytes 196616 | tf_op jit(solution)/shard_map/ppermute | solution.py:41
  12.4 6.8 %collective-permute-start.10 = (f32[32,512]{1,0:T(8,128)S(1)}, f32[32,512]{1,0:T(8,128)S(1)}, u32[]{:S(2)}, u32[]{:S(2)}) collective-permute-start(f32[32,512]{1,0:T(8,128)S(1)} %shard_map.42.refs_4_.refs_5_), channel_id=1, source_target_pairs={{0,6},{1,7},{2,4},{3,5},{4,2},{5,3},{6,0},{7,1},{8,14},{9,15},{10,... | collective-permute-start | bytes 196616 | tf_op jit(solution)/shard_map/ppermute | solution.py:41
  14.9 9.5 %collective-permute-start.12 = (f32[128,512]{1,0:T(8,128)}, f32[128,512]{1,0:T(8,128)S(1)}, u32[]{:S(2)}, u32[]{:S(2)}) collective-permute-start(f32[128,512]{1,0:T(8,128)} %refs_0_), channel_id=1, source_target_pairs={{0,2},{1,3},{2,0},{3,1},{4,6},{5,7},{6,4},{7,5},{8,10},{9,11},{10,... | collective-permute-start | bytes 786440 | tf_op jit(solution)/shard_map/ppermute | solution.py:41
  15.6 12.5 %collective-permute-start.6 = (f32[128,512]{1,0:T(8,128)}, f32[128,512]{1,0:T(8,128)S(1)}, u32[]{:S(2)}, u32[]{:S(2)}) collective-permute-start(f32[128,512]{1,0:T(8,128)} %refs_0_), channel_id=1, source_target_pairs={{0,6},{1,7},{2,4},{3,5},{4,2},{5,3},{6,0},{7,1},{8,14},{9,15},{10,... | collective-permute-start | bytes 786440 | tf_op jit(solution)/shard_map/ppermute | solution.py:41
  16.5 12.1 %collective-permute-start.2 = (f32[128,512]{1,0:T(8,128)}, f32[128,512]{1,0:T(8,128)S(1)}, u32[]{:S(2)}, u32[]{:S(2)}) collective-permute-start(f32[128,512]{1,0:T(8,128)} %refs_0_), channel_id=1, source_target_pairs={{24,0},{16,8},{8,16},{0,24},{25,1},{17,9},{9,17},{1,25},{26,2},{18... | collective-permute-start | bytes 786440 | tf_op jit(solution)/shard_map/ppermute | solution.py:53
  17.0 12.2 %collective-permute-start.1 = (f32[128,512]{1,0:T(8,128)}, f32[128,512]{1,0:T(8,128)S(1)}, u32[]{:S(2)}, u32[]{:S(2)}) collective-permute-start(f32[128,512]{1,0:T(8,128)} %refs_0_), channel_id=1, source_target_pairs={{16,0},{24,8},{0,16},{8,24},{17,1},{25,9},{1,17},{9,25},{18,2},{26... | collective-permute-start | bytes 786440 | tf_op jit(solution)/shard_map/ppermute | solution.py:53
  19.2 9.9 %collective-permute-start = (f32[128,512]{1,0:T(8,128)}, f32[128,512]{1,0:T(8,128)S(1)}, u32[]{:S(2)}, u32[]{:S(2)}) collective-permute-start(f32[128,512]{1,0:T(8,128)} %refs_0_), channel_id=1, source_target_pairs={{8,0},{0,8},{24,16},{16,24},{9,1},{1,9},{25,17},{17,25},{10,2},{2,... | collective-permute-start | bytes 786440 | tf_op jit(solution)/shard_map/ppermute | solution.py:53
  24.4 11.2 %collective-permute-start.14 = (f32[128,512]{1,0:T(8,128)S(1)}, f32[128,512]{1,0:T(8,128)S(1)}, u32[]{:S(2)}, u32[]{:S(2)}) collective-permute-start(f32[128,512]{1,0:T(8,128)S(1)} %collective-permute-done.12.refs_2_), channel_id=1, source_target_pairs={{16,0},{24,8},{0,16},{8,24},{17,1},{25,9},{1,17},{9,25},{18,2},{26... | collective-permute-start | bytes 786440 | tf_op jit(solution)/shard_map/ppermute | solution.py:53
  28.1 11.1 %collective-permute-start.8 = (f32[128,512]{1,0:T(8,128)S(1)}, f32[128,512]{1,0:T(8,128)S(1)}, u32[]{:S(2)}, u32[]{:S(2)}) collective-permute-start(f32[128,512]{1,0:T(8,128)S(1)} %collective-permute-done.6.refs_2_), channel_id=1, source_target_pairs={{16,0},{24,8},{0,16},{8,24},{17,1},{25,9},{1,17},{9,25},{18,2},{26... | collective-permute-start | bytes 786440 | tf_op jit(solution)/shard_map/ppermute | solution.py:53
  32.0 20.1 %collective-permute-start.11 = (f32[544,512]{1,0:T(8,128)S(1)}, f32[544,512]{1,0:T(8,128)S(1)}, u32[]{:S(2)}, u32[]{:S(2)}) collective-permute-start(f32[544,512]{1,0:T(8,128)S(1)} %get-tuple-element.43), channel_id=1, source_target_pairs={{1,0},{0,1},{3,2},{2,3},{5,4},{4,5},{7,6},{6,7},{9,8},{8,9},{11,10... | collective-permute-start | bytes 3342344 | tf_op jit(solution)/shard_map/ppermute | solution.py:45
  32.1 8.7 %collective-permute-start.15 = (f32[128,512]{1,0:T(8,128)S(1)}, f32[128,512]{1,0:T(8,128)S(1)}, u32[]{:S(2)}, u32[]{:S(2)}) collective-permute-start(f32[128,512]{1,0:T(8,128)S(1)} %collective-permute-done.2.refs_3_), channel_id=1, source_target_pairs={{0,2},{1,3},{2,0},{3,1},{4,6},{5,7},{6,4},{7,5},{8,10},{9,11},{10,... | collective-permute-start | bytes 786440 | tf_op jit(solution)/shard_map/ppermute | solution.py:41
  33.1 14.7 %collective-permute-start.9 = (f32[128,512]{1,0:T(8,128)S(1)}, f32[128,512]{1,0:T(8,128)S(1)}, u32[]{:S(2)}, u32[]{:S(2)}) collective-permute-start(f32[128,512]{1,0:T(8,128)S(1)} %collective-permute-done.2.refs_3_), channel_id=1, source_target_pairs={{0,6},{1,7},{2,4},{3,5},{4,2},{5,3},{6,0},{7,1},{8,14},{9,15},{10,... | collective-permute-start | bytes 786440 | tf_op jit(solution)/shard_map/ppermute | solution.py:41
  35.5 22.1 %collective-permute-start.17 = (f32[128,512]{1,0:T(8,128)S(1)}, f32[128,512]{1,0:T(8,128)S(1)}, u32[]{:S(2)}, u32[]{:S(2)}) collective-permute-start(f32[128,512]{1,0:T(8,128)S(1)} %broadcast_select_fusion.3), channel_id=1, source_target_pairs={{1,0},{0,1},{3,2},{2,3},{5,4},{4,5},{7,6},{6,7},{9,8},{8,9},{11,10... | collective-permute-start | bytes 786440 | tf_op jit(solution)/shard_map/ppermute | solution.py:45
  39.2 9.2 %collective-permute-start.13 = (f32[128,512]{1,0:T(8,128)S(1)}, f32[128,512]{1,0:T(8,128)S(1)}, u32[]{:S(2)}, u32[]{:S(2)}) collective-permute-start(f32[128,512]{1,0:T(8,128)S(1)} %collective-permute-done.12.refs_2_), channel_id=1, source_target_pairs={{8,0},{0,8},{24,16},{16,24},{9,1},{1,9},{25,17},{17,25},{10,2},{2,... | collective-permute-start | bytes 786440 | tf_op jit(solution)/shard_map/ppermute | solution.py:53
  40.8 11.3 %collective-permute-start.7 = (f32[128,512]{1,0:T(8,128)S(1)}, f32[128,512]{1,0:T(8,128)S(1)}, u32[]{:S(2)}, u32[]{:S(2)}) collective-permute-start(f32[128,512]{1,0:T(8,128)S(1)} %collective-permute-done.6.refs_2_), channel_id=1, source_target_pairs={{8,0},{0,8},{24,16},{16,24},{9,1},{1,9},{25,17},{17,25},{10,2},{2,... | collective-permute-start | bytes 786440 | tf_op jit(solution)/shard_map/ppermute | solution.py:53
  47.8 9.9 %collective-permute-start.19 = (f32[128,512]{1,0:T(8,128)S(1)}, f32[128,512]{1,0:T(8,128)S(1)}, u32[]{:S(2)}, u32[]{:S(2)}) collective-permute-start(f32[128,512]{1,0:T(8,128)S(1)} %broadcast_select_fusion.1), channel_id=1, source_target_pairs={{1,0},{0,1},{3,2},{2,3},{5,4},{4,5},{7,6},{6,7},{9,8},{8,9},{11,10... | collective-permute-start | bytes 786440 | tf_op jit(solution)/shard_map/ppermute | solution.py:45
  48.4 9.3 %collective-permute-start.20 = (f32[160,512]{1,0:T(8,128)S(1)}, f32[160,512]{1,0:T(8,128)S(1)}, u32[]{:S(2)}, u32[]{:S(2)}) collective-permute-start(f32[160,512]{1,0:T(8,128)S(1)} %pad_maximum_fusion), channel_id=1, source_target_pairs={{1,0},{0,1},{3,2},{2,3},{5,4},{4,5},{7,6},{6,7},{9,8},{8,9},{11,10... | collective-permute-start | bytes 983048 | tf_op jit(solution)/shard_map/ppermute | solution.py:45
  52.1 5.6 %collective-permute-start.18 = (f32[128,512]{1,0:T(8,128)S(1)}, f32[128,512]{1,0:T(8,128)S(1)}, u32[]{:S(2)}, u32[]{:S(2)}) collective-permute-start(f32[128,512]{1,0:T(8,128)S(1)} %broadcast_select_fusion.2), channel_id=1, source_target_pairs={{1,0},{0,1},{3,2},{2,3},{5,4},{4,5},{7,6},{6,7},{9,8},{8,9},{11,10... | collective-permute-start | bytes 786440 | tf_op jit(solution)/shard_map/ppermute | solution.py:45
  60.0 7.6 %collective-permute-start.21 = (f32[32,512]{1,0:T(8,128)S(1)}, f32[32,512]{1,0:T(8,128)S(1)}, u32[]{:S(2)}, u32[]{:S(2)}) collective-permute-start(f32[32,512]{1,0:T(8,128)S(1)} %get-tuple-element.62.refs_4_.refs_6_), channel_id=1, source_target_pairs={{0,6},{1,7},{2,4},{3,5},{4,2},{5,3},{6,0},{7,1},{8,14},{9,15},{10,... | collective-permute-start | bytes 196616 | tf_op jit(solution)/shard_map/ppermute | solution.py:41
  70.3 6.5 %collective-permute-start.25 = (f32[32,512]{1,0:T(8,128)S(1)}, f32[32,512]{1,0:T(8,128)S(1)}, u32[]{:S(2)}, u32[]{:S(2)}) collective-permute-start(f32[32,512]{1,0:T(8,128)S(1)} %shard_map.50.refs_4_.refs_7_), channel_id=1, source_target_pairs={{0,6},{1,7},{2,4},{3,5},{4,2},{5,3},{6,0},{7,1},{8,14},{9,15},{10,... | collective-permute-start | bytes 196616 | tf_op jit(solution)/shard_map/ppermute | solution.py:41
  73.0 13.4 %collective-permute-start.28 = (f32[32,512]{1,0:T(8,128)S(1)}, f32[32,512]{1,0:T(8,128)S(1)}, u32[]{:S(2)}, u32[]{:S(2)}) collective-permute-start(f32[32,512]{1,0:T(8,128)S(1)} %shard_map.50.refs_4_.refs_7_), channel_id=1, source_target_pairs={{1,0},{0,1},{3,2},{2,3},{5,4},{4,5},{7,6},{6,7},{9,8},{8,9},{11,10... | collective-permute-start | bytes 196616 | tf_op jit(solution)/shard_map/ppermute | solution.py:45
  76.9 11.0 %collective-permute-start.27 = (f32[32,512]{1,0:T(8,128)S(1)}, f32[32,512]{1,0:T(8,128)S(1)}, u32[]{:S(2)}, u32[]{:S(2)}) collective-permute-start(f32[32,512]{1,0:T(8,128)S(1)} %broadcast_select_fusion.4), channel_id=1, source_target_pairs={{1,0},{0,1},{3,2},{2,3},{5,4},{4,5},{7,6},{6,7},{9,8},{8,9},{11,10... | collective-permute-start | bytes 196616 | tf_op jit(solution)/shard_map/ppermute | solution.py:45
  88.3 5.1 %collective-permute-start.32 = (f32[32,128]{1,0:T(8,128)S(1)}, f32[32,128]{1,0:T(8,128)S(1)}, u32[]{:S(2)}, u32[]{:S(2)}) collective-permute-start(f32[32,128]{1,0:T(8,128)S(1)} %get-tuple-element.65), channel_id=1, source_target_pairs={{8,0},{0,8},{24,16},{16,24},{9,1},{1,9},{25,17},{17,25},{10,2},{2,... | collective-permute-start | bytes 49160 | tf_op jit(solution)/shard_map/ppermute | solution.py:53
  (13 other events, 42.9 us)

commit v3 on v2

--- a/solution.py
+++ b/solution.py
@@ -99,11 +99,18 @@
     else:
         left_high, left_low = left_high_ref[...], left_low_ref[...]
     high, low = split(normed)
-    part = dot(left_high, high, NN) + dot(left_high, low, NN) + dot(left_low, high, NN)
-    ahead = lax.broadcasted_iota(jnp.int32, (n, n), 1) - lax.broadcasted_iota(jnp.int32, (n, n), 0)
-    shift = 0 if own else offset() * n
-    distance = jnp.abs(ahead + shift).astype(jnp.float32)
-    tapered = part * jnp.maximum(0.0, 1.0 - distance * (1.0 / window))
+    part = dot(
+        jnp.concatenate([left_high, left_high, left_low], 1), jnp.concatenate([high, low, high], 0), NN
+    )
+    column = lax.broadcasted_iota(jnp.int32, (1, n), 1)
+    row = lax.broadcasted_iota(jnp.int32, (n, 1), 0)
+    if own:
+        tapered = part * jnp.maximum(0.0, 1.0 - jnp.abs(column - row).astype(jnp.float32) * (1.0 / window))
+    else:
+        shift = offset()
+        sign = jnp.where(shift > 0, 1, -1)
+        beyond = 1.0 - (sign * (column + shift * n)).astype(jnp.float32) * (1.0 / window)
+        tapered = part * jnp.maximum(0.0, beyond + (sign * row).astype(jnp.float32) * (1.0 / window))
     high, low = split(tapered)
     high_ref[...] = high
     low_ref[...] = low

time: 96.2 us -> 95.4 us (level)
  no operation moved by 1% of the time
where the time goes in v3:
time: 95.4 us; the launch traced here: 95.2 us
  waiting for transfers between devices  45.3 us (47%)
  starting transfers between devices  32.5 us (34%)
  Pallas kernels  14.6 us (15%)
  local copies, waits for them, and re-layouts  1.78 us (2%)
    ppermute x10, waiting for transfers between devices, ring_swap(): return lax.ppermute(block, 'col', route)  22.3 us
    ppermute x10, starting transfers between devices, ring_swap(): return lax.ppermute(block, 'col', route)  16.3 us
    ppermute x13, waiting for transfers between devices, row_xor(): lax.ppermute(block, 'row', [(i ^ mask, i) for i in range(lax.axis_size('r...  14.7 us
    ppermute x13, starting transfers between devices, row_xor(): lax.ppermute(block, 'row', [(i ^ mask, i) for i in range(lax.axis_size('r...  14.3 us
    pallas_call x5, Pallas kernels, gram(): pl.pallas_call(functools.partial(gram_kernel, window, len(pieces), member...  8.55 us
    ppermute x2, waiting for transfers between devices, chip_xor(): lax.ppermute(block, 'col', [(i ^ 2 * mask, i) for i in range(lax.axis_siz...  7.37 us
    pallas_call x6, Pallas kernels, step_call(): pl.pallas_call(kernel, out_shape=outs, compiler_params=vmem_limit(*operan...  3.72 us
  transfers between devices with their start and end apart: 35, of which 20 were waited for; matrix products, arithmetic and copies ran while one was open for 0% of the time, Pallas kernels for 12%

profile of v3, /device:TPU:0, one launch (start us, length us, event | category | flops | bytes accessed | tf_op | source)
XLA Modules:
  0.0 95.2 jit_solution(5997400436424790367)
XLA Ops:
  1.6 3.0 %collective-permute-start.3 = (f32[32,128]{1,0:T(8,128)S(1)}, f32[32,128]{1,0:T(8,128)S(1)}, u32[]{:S(2)}, u32[]{:S(2)}) collective-permute-start(f32[32,128]{1,0:T(8,128)S(1)} %get-tuple-element.37), channel_id=1, source_target_pairs={{8,0},{0,8},{24,16},{16,24},{9,1},{1,9},{25,17},{17,25},{10,2},{2,... | collective-permute-start | bytes 49160 | tf_op jit(solution)/shard_map/ppermute | solution.py:53
  4.6 1.5 %collective-permute-start.4 = (f32[32,128]{1,0:T(8,128)S(1)}, f32[32,128]{1,0:T(8,128)S(1)}, u32[]{:S(2)}, u32[]{:S(2)}) collective-permute-start(f32[32,128]{1,0:T(8,128)S(1)} %get-tuple-element.38), channel_id=1, source_target_pairs={{16,0},{24,8},{0,16},{8,24},{17,1},{25,9},{1,17},{9,25},{18,2},{26... | collective-permute-start | bytes 49160 | tf_op jit(solution)/shard_map/ppermute | solution.py:53
  6.3 2.0 %collective-permute-done.4.refs_2_ = f32[32,128]{1,0:T(8,128)S(1)} collective-permute-done((f32[32,128]{1,0:T(8,128)S(1)}, f32[32,128]{1,0:T(8,128)S(1)}, u32[]{:S(2)}, u32[]{:S(2)}) %collective-permute-start.4) | collective-permute-done | bytes 16416 | tf_op jit(solution)/shard_map/ppermute | solution.py:53
  8.3 2.4 %collective-permute-done.5.refs_3_ = f32[32,128]{1,0:T(8,128)S(1)} collective-permute-done((f32[32,128]{1,0:T(8,128)S(1)}, f32[32,128]{1,0:T(8,128)S(1)}, u32[]{:S(2)}, u32[]{:S(2)}) %collective-permute-start.5) | collective-permute-done | bytes 16416 | tf_op jit(solution)/shard_map/ppermute | solution.py:53
  10.8 1.6 %collective-permute-start.16 = (f32[32,512]{1,0:T(8,128)S(1)}, f32[32,512]{1,0:T(8,128)S(1)}, u32[]{:S(2)}, u32[]{:S(2)}) collective-permute-start(f32[32,512]{1,0:T(8,128)S(1)} %shard_map.42.refs_4_.refs_5_), channel_id=1, source_target_pairs={{0,2},{1,3},{2,0},{3,1},{4,6},{5,7},{6,4},{7,5},{8,10},{9,11},{10,... | collective-permute-start | bytes 196616 | tf_op jit(solution)/shard_map/ppermute | solution.py:41
  12.4 2.5 %collective-permute-start.10 = (f32[32,512]{1,0:T(8,128)S(1)}, f32[32,512]{1,0:T(8,128)S(1)}, u32[]{:S(2)}, u32[]{:S(2)}) collective-permute-start(f32[32,512]{1,0:T(8,128)S(1)} %shard_map.42.refs_4_.refs_5_), channel_id=1, source_target_pairs={{0,6},{1,7},{2,4},{3,5},{4,2},{5,3},{6,0},{7,1},{8,14},{9,15},{10,... | collective-permute-start | bytes 196616 | tf_op jit(solution)/shard_map/ppermute | solution.py:41
  17.0 1.5 %collective-permute-start.1 = (f32[128,512]{1,0:T(8,128)}, f32[128,512]{1,0:T(8,128)S(1)}, u32[]{:S(2)}, u32[]{:S(2)}) collective-permute-start(f32[128,512]{1,0:T(8,128)} %refs_0_), channel_id=1, source_target_pairs={{16,0},{24,8},{0,16},{8,24},{17,1},{25,9},{1,17},{9,25},{18,2},{26... | collective-permute-start | bytes 786440 | tf_op jit(solution)/shard_map/ppermute | solution.py:53
  20.0 4.4 %collective-permute-done.12.refs_2_ = f32[128,512]{1,0:T(8,128)S(1)} collective-permute-done((f32[128,512]{1,0:T(8,128)}, f32[128,512]{1,0:T(8,128)S(1)}, u32[]{:S(2)}, u32[]{:S(2)}) %collective-permute-start.12) | collective-permute-done | bytes 262176 | tf_op jit(solution)/shard_map/ppermute | solution.py:41
  24.9 3.2 %collective-permute-done.6.refs_2_ = f32[128,512]{1,0:T(8,128)S(1)} collective-permute-done((f32[128,512]{1,0:T(8,128)}, f32[128,512]{1,0:T(8,128)S(1)}, u32[]{:S(2)}, u32[]{:S(2)}) %collective-permute-start.6) | collective-permute-done | bytes 262176 | tf_op jit(solution)/shard_map/ppermute | solution.py:41
  30.1 1.9 %shard_map.43 = (bf16[512,512]{1,0:T(8,128)(2,1)S(1)}, bf16[512,512]{1,0:T(8,128)(2,1)S(1)}, f32[32,512]{1,0:T(8,128)S(1)}, f32[8,512]{1,0:T(8,128)S(1)}, bf16[5...) custom-call(f32[128,512]{1,0:T(8,128)S(1)} %copy-done.1, ...), custom_call_target="tpu_custom_call" | custom-call | flops 805306368 | bytes 1048576 | tf_op jit(solution)/shard_map/pallas_call | solution.py:141
  33.1 2.4 %collective-permute-start.9 = (f32[128,512]{1,0:T(8,128)S(1)}, f32[128,512]{1,0:T(8,128)S(1)}, u32[]{:S(2)}, u32[]{:S(2)}) collective-permute-start(f32[128,512]{1,0:T(8,128)S(1)} %collective-permute-done.2.refs_3_), channel_id=1, source_target_pairs={{0,6},{1,7},{2,4},{3,5},{4,2},{5,3},{6,0},{7,1},{8,14},{9,15},{10,... | collective-permute-start | bytes 786440 | tf_op jit(solution)/shard_map/ppermute | solution.py:41
  35.6 3.6 %collective-permute-done.8.refs_4_ = f32[128,512]{1,0:T(8,128)S(1)} collective-permute-done((f32[128,512]{1,0:T(8,128)S(1)}, f32[128,512]{1,0:T(8,128)S(1)}, u32[]{:S(2)}, u32[]{:S(2)}) %collective-permute-start.8) | collective-permute-done | bytes 262176 | tf_op jit(solution)/shard_map/ppermute | solution.py:53
  42.0 5.8 %collective-permute-done.9.refs_5_ = f32[128,512]{1,0:T(8,128)S(1)} collective-permute-done((f32[128,512]{1,0:T(8,128)S(1)}, f32[128,512]{1,0:T(8,128)S(1)}, u32[]{:S(2)}, u32[]{:S(2)}) %collective-permute-start.9) | collective-permute-done | bytes 262176 | tf_op jit(solution)/shard_map/ppermute | solution.py:41
  48.5 3.6 %collective-permute-done.7.refs_3_ = f32[128,512]{1,0:T(8,128)S(1)} collective-permute-done((f32[128,512]{1,0:T(8,128)S(1)}, f32[128,512]{1,0:T(8,128)S(1)}, u32[]{:S(2)}, u32[]{:S(2)}) %collective-permute-start.7) | collective-permute-done | bytes 262176 | tf_op jit(solution)/shard_map/ppermute | solution.py:53
  53.6 1.7 %shard_map.45 = (bf16[512,512]{1,0:T(8,128)(2,1)S(1)}, bf16[512,512]{1,0:T(8,128)(2,1)S(1)}, f32[32,512]{1,0:T(8,128)S(1)}, f32[8,512]{1,0:T(8,128)S(1)}) custom-call(bf16[512,512]{1,0:T(8,128)(2,1)S(1)} %get-tuple-element.41.refs_0_, bf16[512,512]{1,0:T(8,128)(2,1)S(1)} %get-tuple-element.42.refs_1_, f32[128,512]{1,0:T(8,128)S(1)} %collective-permute-done.6.refs_2_, ...), custom_call_target="tpu_custom_call" | custom-call | flops 805306368 | bytes 1048576 | tf_op jit(solution)/shard_map/pallas_call | solution.py:141
  55.4 1.7 %shard_map.46 = (bf16[512,512]{1,0:T(8,128)(2,1)S(1)}, bf16[512,512]{1,0:T(8,128)(2,1)S(1)}, f32[32,512]{1,0:T(8,128)S(1)}, f32[8,512]{1,0:T(8,128)S(1)}) custom-call(bf16[512,512]{1,0:T(8,128)(2,1)S(1)} %get-tuple-element.41.refs_0_, bf16[512,512]{1,0:T(8,128)(2,1)S(1)} %get-tuple-element.42.refs_1_, f32[128,512]{1,0:T(8,128)S(1)} %collective-permute-done.12.refs_2_, ...), custom_call_target="tpu_custom_call" | custom-call | flops 805306368 | bytes 1048576 | tf_op jit(solution)/shard_map/pallas_call | solution.py:141
  57.2 1.7 %shard_map.47 = (bf16[512,512]{1,0:T(8,128)(2,1)S(1)}, bf16[512,512]{1,0:T(8,128)(2,1)S(1)}, f32[32,512]{1,0:T(8,128)S(1)}, f32[8,128]{1,0:T(8,128)S(1)}) custom-call(bf16[512,512]{1,0:T(8,128)(2,1)S(1)} %get-tuple-element.41.refs_0_, bf16[512,512]{1,0:T(8,128)(2,1)S(1)} %get-tuple-element.42.refs_1_, f32[128,512]{1,0:T(8,128)S(1)} %collective-permute-done.17.refs_2_, ...), custom_call_target="tpu_custom_call" | custom-call | flops 805306368 | bytes 1048576 | tf_op jit(solution)/shard_map/pallas_call | solution.py:141
  59.3 3.4 %collective-permute-start.21 = (f32[32,512]{1,0:T(8,128)S(1)}, f32[32,512]{1,0:T(8,128)S(1)}, u32[]{:S(2)}, u32[]{:S(2)}) collective-permute-start(f32[32,512]{1,0:T(8,128)S(1)} %get-tuple-element.62.refs_4_.refs_6_), channel_id=1, source_target_pairs={{0,6},{1,7},{2,4},{3,5},{4,2},{5,3},{6,0},{7,1},{8,14},{9,15},{10,... | collective-permute-start | bytes 196616 | tf_op jit(solution)/shard_map/ppermute | solution.py:41
  63.4 3.4 %collective-permute-done.21.refs_4_ = f32[32,512]{1,0:T(8,128)S(1)} collective-permute-done((f32[32,512]{1,0:T(8,128)S(1)}, f32[32,512]{1,0:T(8,128)S(1)}, u32[]{:S(2)}, u32[]{:S(2)}) %collective-permute-start.21) | collective-permute-done | bytes 65568 | tf_op jit(solution)/shard_map/ppermute | solution.py:41
  69.6 2.6 %collective-permute-start.25 = (f32[32,512]{1,0:T(8,128)S(1)}, f32[32,512]{1,0:T(8,128)S(1)}, u32[]{:S(2)}, u32[]{:S(2)}) collective-permute-start(f32[32,512]{1,0:T(8,128)S(1)} %shard_map.50.refs_4_.refs_7_), channel_id=1, source_target_pairs={{0,6},{1,7},{2,4},{3,5},{4,2},{5,3},{6,0},{7,1},{8,14},{9,15},{10,... | collective-permute-start | bytes 196616 | tf_op jit(solution)/shard_map/ppermute | solution.py:41
  73.3 2.8 %collective-permute-done.25.refs_4_ = f32[32,512]{1,0:T(8,128)S(1)} collective-permute-done((f32[32,512]{1,0:T(8,128)S(1)}, f32[32,512]{1,0:T(8,128)S(1)}, u32[]{:S(2)}, u32[]{:S(2)}) %collective-permute-start.25) | collective-permute-done | bytes 65568 | tf_op jit(solution)/shard_map/ppermute | solution.py:41
  77.5 3.6 %collective-permute-done.30 = f32[8,128]{1,0:T(8,128)S(1)} collective-permute-done((f32[8,128]{1,0:T(8,128)S(1)}, f32[8,128]{1,0:T(8,128)S(1)}, u32[]{:S(2)}, u32[]{:S(2)}) %collective-permute-start.30) | collective-permute-done | bytes 4128 | tf_op jit(solution)/shard_map/ppermute | solution.py:49
  81.9 3.8 %collective-permute-done.31 = f32[8,128]{1,0:T(8,128)S(1)} collective-permute-done((f32[8,128]{1,0:T(8,128)S(1)}, f32[8,128]{1,0:T(8,128)S(1)}, u32[]{:S(2)}, u32[]{:S(2)}) %collective-permute-start.31) | collective-permute-done | bytes 4128 | tf_op jit(solution)/shard_map/ppermute | solution.py:49
  92.7 1.8 %collective-permute-done.34.refs_3_ = f32[32,128]{1,0:T(8,128)S(1)} collective-permute-done((f32[32,128]{1,0:T(8,128)S(1)}, f32[32,128]{1,0:T(8,128)S(1)}, u32[]{:S(2)}, u32[]{:S(2)}) %collective-permute-start.34) | collective-permute-done | bytes 16416 | tf_op jit(solution)/shard_map/ppermute | solution.py:53
  (76 shorter events, 28.3 us)
Async XLA Ops:
  1.6 4.8 %collective-permute-start.3 = (f32[32,128]{1,0:T(8,128)S(1)}, f32[32,128]{1,0:T(8,128)S(1)}, u32[]{:S(2)}, u32[]{:S(2)}) collective-permute-start(f32[32,128]{1,0:T(8,128)S(1)} %get-tuple-element.37), channel_id=1, source_target_pairs={{8,0},{0,8},{24,16},{16,24},{9,1},{1,9},{25,17},{17,25},{10,2},{2,... | collective-permute-start | bytes 49160 | tf_op jit(solution)/shard_map/ppermute | solution.py:53
  10.8 6.2 %collective-permute-start.16 = (f32[32,512]{1,0:T(8,128)S(1)}, f32[32,512]{1,0:T(8,128)S(1)}, u32[]{:S(2)}, u32[]{:S(2)}) collective-permute-start(f32[32,512]{1,0:T(8,128)S(1)} %shard_map.42.refs_4_.refs_5_), channel_id=1, source_target_pairs={{0,2},{1,3},{2,0},{3,1},{4,6},{5,7},{6,4},{7,5},{8,10},{9,11},{10,... | collective-permute-start | bytes 196616 | tf_op jit(solution)/shard_map/ppermute | solution.py:41
  12.4 6.8 %collective-permute-start.10 = (f32[32,512]{1,0:T(8,128)S(1)}, f32[32,512]{1,0:T(8,128)S(1)}, u32[]{:S(2)}, u32[]{:S(2)}) collective-permute-start(f32[32,512]{1,0:T(8,128)S(1)} %shard_map.42.refs_4_.refs_5_), channel_id=1, source_target_pairs={{0,6},{1,7},{2,4},{3,5},{4,2},{5,3},{6,0},{7,1},{8,14},{9,15},{10,... | collective-permute-start | bytes 196616 | tf_op jit(solution)/shard_map/ppermute | solution.py:41
  14.9 9.5 %collective-permute-start.12 = (f32[128,512]{1,0:T(8,128)}, f32[128,512]{1,0:T(8,128)S(1)}, u32[]{:S(2)}, u32[]{:S(2)}) collective-permute-start(f32[128,512]{1,0:T(8,128)} %refs_0_), channel_id=1, source_target_pairs={{0,2},{1,3},{2,0},{3,1},{4,6},{5,7},{6,4},{7,5},{8,10},{9,11},{10,... | collective-permute-start | bytes 786440 | tf_op jit(solution)/shard_map/ppermute | solution.py:41
  15.6 12.5 %collective-permute-start.6 = (f32[128,512]{1,0:T(8,128)}, f32[128,512]{1,0:T(8,128)S(1)}, u32[]{:S(2)}, u32[]{:S(2)}) collective-permute-start(f32[128,512]{1,0:T(8,128)} %refs_0_), channel_id=1, source_target_pairs={{0,6},{1,7},{2,4},{3,5},{4,2},{5,3},{6,0},{7,1},{8,14},{9,15},{10,... | collective-permute-start | bytes 786440 | tf_op jit(solution)/shard_map/ppermute | solution.py:41
  16.5 12.1 %collective-permute-start.2 = (f32[128,512]{1,0:T(8,128)}, f32[128,512]{1,0:T(8,128)S(1)}, u32[]{:S(2)}, u32[]{:S(2)}) collective-permute-start(f32[128,512]{1,0:T(8,128)} %refs_0_), channel_id=1, source_target_pairs={{24,0},{16,8},{8,16},{0,24},{25,1},{17,9},{9,17},{1,25},{26,2},{18... | collective-permute-start | bytes 786440 | tf_op jit(solution)/shard_map/ppermute | solution.py:53
  17.0 12.2 %collective-permute-start.1 = (f32[128,512]{1,0:T(8,128)}, f32[128,512]{1,0:T(8,128)S(1)}, u32[]{:S(2)}, u32[]{:S(2)}) collective-permute-start(f32[128,512]{1,0:T(8,128)} %refs_0_), channel_id=1, source_target_pairs={{16,0},{24,8},{0,16},{8,24},{17,1},{25,9},{1,17},{9,25},{18,2},{26... | collective-permute-start | bytes 786440 | tf_op jit(solution)/shard_map/ppermute | solution.py:53
  19.2 9.9 %collective-permute-start = (f32[128,512]{1,0:T(8,128)}, f32[128,512]{1,0:T(8,128)S(1)}, u32[]{:S(2)}, u32[]{:S(2)}) collective-permute-start(f32[128,512]{1,0:T(8,128)} %refs_0_), channel_id=1, source_target_pairs={{8,0},{0,8},{24,16},{16,24},{9,1},{1,9},{25,17},{17,25},{10,2},{2,... | collective-permute-start | bytes 786440 | tf_op jit(solution)/shard_map/ppermute | solution.py:53
  24.4 11.2 %collective-permute-start.14 = (f32[128,512]{1,0:T(8,128)S(1)}, f32[128,512]{1,0:T(8,128)S(1)}, u32[]{:S(2)}, u32[]{:S(2)}) collective-permute-start(f32[128,512]{1,0:T(8,128)S(1)} %collective-permute-done.12.refs_2_), channel_id=1, source_target_pairs={{16,0},{24,8},{0,16},{8,24},{17,1},{25,9},{1,17},{9,25},{18,2},{26... | collective-permute-start | bytes 786440 | tf_op jit(solution)/shard_map/ppermute | solution.py:53
  28.1 11.1 %collective-permute-start.8 = (f32[128,512]{1,0:T(8,128)S(1)}, f32[128,512]{1,0:T(8,128)S(1)}, u32[]{:S(2)}, u32[]{:S(2)}) collective-permute-start(f32[128,512]{1,0:T(8,128)S(1)} %collective-permute-done.6.refs_2_), channel_id=1, source_target_pairs={{16,0},{24,8},{0,16},{8,24},{17,1},{25,9},{1,17},{9,25},{18,2},{26... | collective-permute-start | bytes 786440 | tf_op jit(solution)/shard_map/ppermute | solution.py:53
  32.0 20.2 %collective-permute-start.11 = (f32[544,512]{1,0:T(8,128)S(1)}, f32[544,512]{1,0:T(8,128)S(1)}, u32[]{:S(2)}, u32[]{:S(2)}) collective-permute-start(f32[544,512]{1,0:T(8,128)S(1)} %get-tuple-element.43), channel_id=1, source_target_pairs={{1,0},{0,1},{3,2},{2,3},{5,4},{4,5},{7,6},{6,7},{9,8},{8,9},{11,10... | collective-permute-start | bytes 3342344 | tf_op jit(solution)/shard_map/ppermute | solution.py:45
  32.0 8.7 %collective-permute-start.15 = (f32[128,512]{1,0:T(8,128)S(1)}, f32[128,512]{1,0:T(8,128)S(1)}, u32[]{:S(2)}, u32[]{:S(2)}) collective-permute-start(f32[128,512]{1,0:T(8,128)S(1)} %collective-permute-done.2.refs_3_), channel_id=1, source_target_pairs={{0,2},{1,3},{2,0},{3,1},{4,6},{5,7},{6,4},{7,5},{8,10},{9,11},{10,... | collective-permute-start | bytes 786440 | tf_op jit(solution)/shard_map/ppermute | solution.py:41
  33.1 14.7 %collective-permute-start.9 = (f32[128,512]{1,0:T(8,128)S(1)}, f32[128,512]{1,0:T(8,128)S(1)}, u32[]{:S(2)}, u32[]{:S(2)}) collective-permute-start(f32[128,512]{1,0:T(8,128)S(1)} %collective-permute-done.2.refs_3_), channel_id=1, source_target_pairs={{0,6},{1,7},{2,4},{3,5},{4,2},{5,3},{6,0},{7,1},{8,14},{9,15},{10,... | collective-permute-start | bytes 786440 | tf_op jit(solution)/shard_map/ppermute | solution.py:41
  35.5 21.6 %collective-permute-start.17 = (f32[128,512]{1,0:T(8,128)S(1)}, f32[128,512]{1,0:T(8,128)S(1)}, u32[]{:S(2)}, u32[]{:S(2)}) collective-permute-start(f32[128,512]{1,0:T(8,128)S(1)} %broadcast_select_fusion.3), channel_id=1, source_target_pairs={{1,0},{0,1},{3,2},{2,3},{5,4},{4,5},{7,6},{6,7},{9,8},{8,9},{11,10... | collective-permute-start | bytes 786440 | tf_op jit(solution)/shard_map/ppermute | solution.py:45
  39.2 9.2 %collective-permute-start.13 = (f32[128,512]{1,0:T(8,128)S(1)}, f32[128,512]{1,0:T(8,128)S(1)}, u32[]{:S(2)}, u32[]{:S(2)}) collective-permute-start(f32[128,512]{1,0:T(8,128)S(1)} %collective-permute-done.12.refs_2_), channel_id=1, source_target_pairs={{8,0},{0,8},{24,16},{16,24},{9,1},{1,9},{25,17},{17,25},{10,2},{2,... | collective-permute-start | bytes 786440 | tf_op jit(solution)/shard_map/ppermute | solution.py:53
  40.7 11.3 %collective-permute-start.7 = (f32[128,512]{1,0:T(8,128)S(1)}, f32[128,512]{1,0:T(8,128)S(1)}, u32[]{:S(2)}, u32[]{:S(2)}) collective-permute-start(f32[128,512]{1,0:T(8,128)S(1)} %collective-permute-done.6.refs_2_), channel_id=1, source_target_pairs={{8,0},{0,8},{24,16},{16,24},{9,1},{1,9},{25,17},{17,25},{10,2},{2,... | collective-permute-start | bytes 786440 | tf_op jit(solution)/shard_map/ppermute | solution.py:53
  47.8 9.3 %collective-permute-start.19 = (f32[128,512]{1,0:T(8,128)S(1)}, f32[128,512]{1,0:T(8,128)S(1)}, u32[]{:S(2)}, u32[]{:S(2)}) collective-permute-start(f32[128,512]{1,0:T(8,128)S(1)} %broadcast_select_fusion.1), channel_id=1, source_target_pairs={{1,0},{0,1},{3,2},{2,3},{5,4},{4,5},{7,6},{6,7},{9,8},{8,9},{11,10... | collective-permute-start | bytes 786440 | tf_op jit(solution)/shard_map/ppermute | solution.py:45
  48.4 8.8 %collective-permute-start.20 = (f32[160,512]{1,0:T(8,128)S(1)}, f32[160,512]{1,0:T(8,128)S(1)}, u32[]{:S(2)}, u32[]{:S(2)}) collective-permute-start(f32[160,512]{1,0:T(8,128)S(1)} %pad_maximum_fusion), channel_id=1, source_target_pairs={{1,0},{0,1},{3,2},{2,3},{5,4},{4,5},{7,6},{6,7},{9,8},{8,9},{11,10... | collective-permute-start | bytes 983048 | tf_op jit(solution)/shard_map/ppermute | solution.py:45
  52.1 5.1 %collective-permute-start.18 = (f32[128,512]{1,0:T(8,128)S(1)}, f32[128,512]{1,0:T(8,128)S(1)}, u32[]{:S(2)}, u32[]{:S(2)}) collective-permute-start(f32[128,512]{1,0:T(8,128)S(1)} %broadcast_select_fusion.2), channel_id=1, source_target_pairs={{1,0},{0,1},{3,2},{2,3},{5,4},{4,5},{7,6},{6,7},{9,8},{8,9},{11,10... | collective-permute-start | bytes 786440 | tf_op jit(solution)/shard_map/ppermute | solution.py:45
  59.3 7.5 %collective-permute-start.21 = (f32[32,512]{1,0:T(8,128)S(1)}, f32[32,512]{1,0:T(8,128)S(1)}, u32[]{:S(2)}, u32[]{:S(2)}) collective-permute-start(f32[32,512]{1,0:T(8,128)S(1)} %get-tuple-element.62.refs_4_.refs_6_), channel_id=1, source_target_pairs={{0,6},{1,7},{2,4},{3,5},{4,2},{5,3},{6,0},{7,1},{8,14},{9,15},{10,... | collective-permute-start | bytes 196616 | tf_op jit(solution)/shard_map/ppermute | solution.py:41
  69.6 6.5 %collective-permute-start.25 = (f32[32,512]{1,0:T(8,128)S(1)}, f32[32,512]{1,0:T(8,128)S(1)}, u32[]{:S(2)}, u32[]{:S(2)}) collective-permute-start(f32[32,512]{1,0:T(8,128)S(1)} %shard_map.50.refs_4_.refs_7_), channel_id=1, source_target_pairs={{0,6},{1,7},{2,4},{3,5},{4,2},{5,3},{6,0},{7,1},{8,14},{9,15},{10,... | collective-permute-start | bytes 196616 | tf_op jit(solution)/shard_map/ppermute | solution.py:41
  72.2 13.4 %collective-permute-start.28 = (f32[32,512]{1,0:T(8,128)S(1)}, f32[32,512]{1,0:T(8,128)S(1)}, u32[]{:S(2)}, u32[]{:S(2)}) collective-permute-start(f32[32,512]{1,0:T(8,128)S(1)} %shard_map.50.refs_4_.refs_7_), channel_id=1, source_target_pairs={{1,0},{0,1},{3,2},{2,3},{5,4},{4,5},{7,6},{6,7},{9,8},{8,9},{11,10... | collective-permute-start | bytes 196616 | tf_op jit(solution)/shard_map/ppermute | solution.py:45
  76.1 11.0 %collective-permute-start.27 = (f32[32,512]{1,0:T(8,128)S(1)}, f32[32,512]{1,0:T(8,128)S(1)}, u32[]{:S(2)}, u32[]{:S(2)}) collective-permute-start(f32[32,512]{1,0:T(8,128)S(1)} %broadcast_select_fusion.4), channel_id=1, source_target_pairs={{1,0},{0,1},{3,2},{2,3},{5,4},{4,5},{7,6},{6,7},{9,8},{8,9},{11,10... | collective-permute-start | bytes 196616 | tf_op jit(solution)/shard_map/ppermute | solution.py:45
  87.6 5.1 %collective-permute-start.32 = (f32[32,128]{1,0:T(8,128)S(1)}, f32[32,128]{1,0:T(8,128)S(1)}, u32[]{:S(2)}, u32[]{:S(2)}) collective-permute-start(f32[32,128]{1,0:T(8,128)S(1)} %get-tuple-element.65), channel_id=1, source_target_pairs={{8,0},{0,8},{24,16},{16,24},{9,1},{1,9},{25,17},{17,25},{10,2},{2,... | collective-permute-start | bytes 49160 | tf_op jit(solution)/shard_map/ppermute | solution.py:53
  (13 other events, 42.9 us)
